TPU v7x, 256 devices: a whole 4x4x8 slice. The times are simulated.
256 devices in a mesh: dp: 16 (over y_hi, z), lon: 16 (over x, y_lo, core).
Axes of the slice: x: 4, y: 4 (y_hi: 2, y_lo: 2; y = y_hi * 2 + y_lo), z: 8, core: 2. Of those that a mesh axis runs over, the one named last changes fastest.
Arguments:
- fields: bfloat16 [16, 16, 2048, 192], P('dp', None, 'lon'), may hold values from -6 to 6
- cotangent: bfloat16 [16, 16, 2048, 192], P('dp', None, 'lon'), may hold values from -6 to 6
- land_sea: int32 [16, 2048], P(None, 'lon'), may hold values 0 or 1
- kernel: float32 [7, 7, 192], replicated, may hold values from -0.875 to 0.875
- ln_gain: float32 [192], replicated, may hold values from 0.5 to 1.5
- weight_in: bfloat16 [192, 768], replicated, may hold values from -0.4375 to 0.4375
- bias_in: float32 [768], replicated, may hold values from -3 to 3
- weight_out: bfloat16 [768, 192], replicated, may hold values from -0.21875 to 0.21875
Outputs:
- output: bfloat16 [16, 16, 2048, 192], P('dp', None, 'lon')
- grad_fields: bfloat16 [16, 16, 2048, 192], P('dp', None, 'lon')
- grad_in: float32 [192, 768], P('dp')
- grad_out: float32 [768, 192], P('dp')
- grad_kernel: float32 [7, 7, 192], replicated
- grad_gain: float32 [192], replicated
- grad_bias: float32 [768], replicated
All inputs are finite; a program needn't handle non-finite values. No bound on the sum of `land_sea` on one device may be relied on, other than what follows from the above.
Results may differ from a plain program's by a relative error of at most 0.025.
Values may be sent and summed in bfloat16 or wider, within the bound.
A program may use at most 64 MiB of HBM per device.

v0:
```python
import math

import jax
import jax.numpy as jnp
from jax import lax
from jax.sharding import PartitionSpec as P


def extended(x, sides, width):
    for axis, dim in sides:
        peers, length = (lax.axis_size(axis), x.shape[dim])
        up = [(i, (i + 1) % peers) for i in range(peers)]
        down = [(j, i) for i, j in up]
        last = lax.slice_in_dim(x, length - width, length, axis=dim)
        first = lax.slice_in_dim(x, 0, width, axis=dim)
        before = lax.ppermute(last, axis, up)
        after = lax.ppermute(first, axis, down)
        x = jnp.concatenate([before, x, after], axis=dim)
    return x


def gelu_exact(value):
    return value * (1.0 + lax.erf(value / math.sqrt(2.0))) / 2.0


def gelu_slope(value):
    return (1.0 + lax.erf(value / math.sqrt(2.0))) / 2.0 + value * jnp.exp(
        -value * value / 2.0
    ) / math.sqrt(2.0 * math.pi)


def pad_rows(block):
    return jnp.pad(block, ((0, 0), (3, 3), (0, 0), (0, 0)))


def depthwise(padded, kernel, lat_rows, lon_cols):
    total = jnp.zeros((padded.shape[0], lat_rows, lon_cols, padded.shape[3]), jnp.float32)
    for row_off in range(7):
        for col_off in range(7):
            total = (
                total
                + padded[:, row_off : row_off + lat_rows, col_off : col_off + lon_cols].astype(
                    jnp.float32
                )
                * kernel[row_off, col_off]
            )
    return total


def transposed(padded, kernel, lat_rows, lon_cols):
    total = jnp.zeros((padded.shape[0], lat_rows, lon_cols, padded.shape[3]), jnp.float32)
    for row_off in range(7):
        for col_off in range(7):
            total = (
                total
                + padded[
                    :, 6 - row_off : 6 - row_off + lat_rows, 6 - col_off : 6 - col_off + lon_cols
                ].astype(jnp.float32)
                * kernel[row_off, col_off]
            )
    return total


def kernel_terms(padded, d_conv, lat_rows, lon_cols):
    d_float = d_conv.astype(jnp.float32)
    rows_out = []
    for row_off in range(7):
        cols_out = []
        for col_off in range(7):
            window = padded[:, row_off : row_off + lat_rows, col_off : col_off + lon_cols].astype(
                jnp.float32
            )
            cols_out.append(jnp.sum(window * d_float, axis=(0, 1, 2)))
        rows_out.append(jnp.stack(cols_out, axis=0))
    return jnp.stack(rows_out, axis=0)


def per_device(fields, cotangent, land_sea, kernel, ln_gain, weight_in, bias_in, weight_out):
    samples_here, lat_rows, lon_cols, channels = fields.shape
    mask_b = land_sea.astype(jnp.bfloat16)[None, :, :, None]
    mask_f = mask_b.astype(jnp.float32)
    masked = fields * mask_b
    padded = pad_rows(extended(masked, (("lon", 2),), 3))
    conv = depthwise(padded, kernel, lat_rows, lon_cols)
    mean_c = jnp.mean(conv, axis=-1, keepdims=True)
    centered = conv - mean_c
    inv_sigma = lax.rsqrt(jnp.mean(centered * centered, axis=-1, keepdims=True) + 1e-06)
    nhat = centered * inv_sigma
    normed = (nhat * ln_gain).astype(jnp.bfloat16)
    flat = normed.reshape(-1, channels)
    pre = jnp.dot(flat, weight_in, preferred_element_type=jnp.float32) + bias_in
    act = gelu_exact(pre).astype(jnp.bfloat16)
    branch = jnp.dot(act, weight_out, preferred_element_type=jnp.float32).reshape(fields.shape)
    output = (mask_f * (fields.astype(jnp.float32) + branch)).astype(jnp.bfloat16)
    grad_m = cotangent * mask_b
    grad_flat = grad_m.reshape(-1, channels)
    d_act = lax.dot_general(
        grad_flat, weight_out, (((1,), (1,)), ((), ())), preferred_element_type=jnp.float32
    )
    d_pre = (d_act * gelu_slope(pre)).astype(jnp.bfloat16)
    part_out = lax.dot_general(
        act, grad_flat, (((0,), (0,)), ((), ())), preferred_element_type=jnp.float32
    )
    part_in = lax.dot_general(
        flat, d_pre, (((0,), (0,)), ((), ())), preferred_element_type=jnp.float32
    )
    part_bias = jnp.sum(d_pre.astype(jnp.float32), axis=0)
    d_normed = lax.dot_general(
        d_pre, weight_in, (((1,), (1,)), ((), ())), preferred_element_type=jnp.float32
    ).reshape(conv.shape)
    part_gain = jnp.sum(d_normed * nhat, axis=(0, 1, 2))
    d_hat = d_normed * ln_gain
    d_conv = (
        inv_sigma
        * (
            d_hat
            - jnp.mean(d_hat, axis=-1, keepdims=True)
            - nhat * jnp.mean(d_hat * nhat, axis=-1, keepdims=True)
        )
    ).astype(jnp.bfloat16)
    part_kernel = kernel_terms(padded, d_conv, lat_rows, lon_cols)
    grad_pad = pad_rows(extended(d_conv, (("lon", 2),), 3))
    spread = transposed(grad_pad, kernel, lat_rows, lon_cols)
    grad_fields = (grad_m.astype(jnp.float32) + mask_f * spread).astype(jnp.bfloat16)
    summed_in, summed_out = (
        lax.psum(part_in.astype(jnp.bfloat16), "lon").astype(jnp.float32),
        lax.psum(part_out.astype(jnp.bfloat16), "lon").astype(jnp.float32),
    )
    summed_in, summed_out = (
        lax.psum_scatter(
            summed_in.astype(jnp.bfloat16), "dp", scatter_dimension=0, tiled=True
        ).astype(jnp.float32),
        lax.psum_scatter(
            summed_out.astype(jnp.bfloat16), "dp", scatter_dimension=0, tiled=True
        ).astype(jnp.float32),
    )
    sum_kernel, sum_gain, sum_bias = lax.psum((part_kernel, part_gain, part_bias), ("dp", "lon"))
    scale = 1.0 / math.sqrt(
        samples_here * lat_rows * lon_cols * lax.axis_size("dp") * lax.axis_size("lon")
    )
    return (
        output,
        grad_fields,
        summed_in * scale,
        summed_out * scale,
        sum_kernel * scale,
        sum_gain * scale,
        sum_bias * scale,
    )


def solution(mesh):
    placed = (
        P("dp", None, "lon", None),
        P("dp", None, "lon", None),
        P(None, "lon"),
        P(),
        P(),
        P(),
        P(),
        P(),
    )
    return jax.shard_map(
        per_device,
        mesh=mesh,
        in_specs=placed,
        out_specs=(
            P("dp", None, "lon", None),
            P("dp", None, "lon", None),
            P("dp", None),
            P("dp", None),
            P(),
            P(),
            P(),
        ),
        check_vma=False,
    )
```

profile of v0, /device:TPU:1, one launch (start us, length us, event | category | flops | bytes accessed | tf_op | source)
XLA Modules:
  0.0 518.3 jit_solution(5383813280703782984)
XLA Ops:
  7.2 2.7 copy.41
  11.3 0.9 copy.36
  12.2 2.0 broadcast_multiply_fusion
  14.2 3.3 collective-permute-start.1
  19.1 0.8 copy.35
  19.9 1.9 copy.42
  23.1 0.9 select_maximum_fusion.2
  24.3 19.4 %fusion.149 = (f32[16,128]{0,1:T(8,128)S(1)}, f32[1,16,128,192]{3,1,2,0:T(8,128)S(1)}) fusion(f32[192]{0:T(256)} %bitcast.48, bf16[1,22,134,192]{3,1,2,0:T(8,128)(2,1)S(1)} %select_maximum_fusion.2, f32[192]{0:T(256)} %bitcast.47, f32[192]{0:T(256)S(1)} %bitcast.167, f32[192]{0:T(256)S(1)} %bitcast.169, f32[192]{0:T(256)S(1)} %bitcast.171, ...), kind=kLoop, calls=%fused_computation.300 | loop fusion | flops 60160000 | bytes 35472128 | tf_op jit(solution)/shard_map/reduce_sum | solution.py:85
  45.8 1.9 copy.39
  47.7 4.2 multiply_convert_fusion
  51.9 4.6 convert_reduce_fusion
  56.5 2.4 multiply_reduce_fusion.3
  58.9 1.5 convolution_convert_fusion.1
  60.4 41.1 %fusion = bf16[16,768]{1,0:T(8,128)(2,1)} fusion(bf16[192,768]{1,0:T(8,128)(2,1)} %convolution_convert_fusion.1), kind=kCustom, calls=%all-reduce-scatter | all-reduce-scatter fusion | flops 196609 | bytes 320512
  101.5 1.9 collective-permute-start.6
  103.4 1.9 collective-permute-start.5
  105.3 1.9 collective-permute-start.4
  107.2 4.4 convolution_bitcast_fusion
  111.5 1.8 convolution_convert_fusion
  113.3 2.8 copy.51
  116.2 3.0 copy.43
  119.2 3.3 multiply_reduce_fusion
  122.6 9.4 %fusion.129 = (f32[192]{0:T(256)}, f32[192]{0:T(256)}, f32[192]{0:T(256)}, f32[192]{0:T(256)}, f32[192]{0:T(256)}, /*index=5*/f32[192]{0:T(256)}, f32[192]{0:T(2...) fusion(bf16[1,22,134,192]{3,1,2,0:T(8,128)(2,1)S(1)} %select_ma, ...), kind=kLoop, calls=%fused_computation.233 | loop fusion | flops 24769152 | bytes 18135296 | tf_op jit(solution)/shard_map/reduce_sum | solution.py:73
  132.6 2.7 fusion.128
  135.3 7.3 %fusion.130 = (f32[192]{0:T(256)}, f32[192]{0:T(256)}, f32[192]{0:T(256)}, f32[192]{0:T(256)}, f32[192]{0:T(256)}, /*index=5*/f32[192]{0:T(256)}, f32[192]{0:T(2...) fusion(bf16[1,16,128,192]{3,1,2,0:T(8,128)(2,1)S(1)} %get-tuple, ...), kind=kLoop, calls=%fused_computation.234 | loop fusion | flops 21623424 | bytes 14956032 | tf_op jit(solution)/shard_map/reduce_sum | solution.py:73
  142.7 1.5 copy.49
  144.2 3.2 copy.40
  147.4 7.6 %collective-permute-start.2 = (bf16[1,16,3,192]{3,1,2,0:T(8,128)(2,1)}, bf16[1,16,3,192]{3,1,2,0:T(8,128)(2,1)}, u32[]{:S(2)}, u32[]{:S(2)}) collective-permute-start(bf16[1,16,3,192]{3,1,2,0:T(8,128)(2,1)} %get-tuple-element.84), channel_id=1, source_target_pairs={{0,1},{1,2},{2,3},{3,4},{4,5},{5,6},{6,7},{7,8},{8,9},{9,10},{10,1... | collective-permute-start | bytes 55304 | tf_op jit(solution)/shard_map/ppermute | solution.py:16
  155.0 1.8 collective-permute-start.3
  156.9 1.3 stack.199
  158.2 1.3 constant_dynamic-update-slice_fusion.6
  159.5 1.3 stack.208
  160.8 1.3 constant_dynamic-update-slice_fusion.5
  162.1 1.3 stack.217
  163.4 1.3 constant_dynamic-update-slice_fusion.4
  164.7 5.5 %fusion.109 = (f32[192]{0:T(256)}, f32[192]{0:T(256)}, f32[192]{0:T(256)}, f32[192]{0:T(256)}, f32[192]{0:T(256)}, /*index=5*/f32[192]{0:T(256)}, f32[192]{0:T(256)}) fusion(bf16[1,16,128,192]{3,1,2,0:T(8,128)(2,1)S(1)} %get-tuple-element.80, bf16[1,16,3,192]{3,1,2,0:T(8,128)(2,1)S(1)} %collective-permute-done.1, ...), kind=kLoop, calls=%fused_computation.213 | loop fusion | flops 11008704 | bytes 1615104 | tf_op jit(solution)/shard_map/reduce_sum | solution.py:73
  170.2 0.7 stack.226
  175.5 80.1 %all-reduce.4 = (f32[7,7,192]{2,1,0:T(8,128)S(1)}, f32[192]{0:T(256)S(1)}, f32[768]{0:T(1024)S(1)}) all-reduce(f32[7,7,192]{2,1,0:T(8,128)} %constant_dynamic-update-slice_fusion, f32[192]{0:T(256)} %get-tuple-element.21, f32[768]{0:T(1024)} %get-tuple-element.142), channel_id=1, replica_groups=mesh['dp'=16,'lon'=16] {'dp','lon'}, use_global_device_ids=true, to_apply=%region_57.58 | all-reduce | flops 10368 | bytes 82944 | tf_op jit(solution)/shard_map/psum | solution.py:137
  256.9 1.9 multiply_convert_fusion.2
  259.4 0.7 slice.826
  260.1 1.6 copy.46
  261.8 5.2 collective-permute-start.7
  267.0 1.6 select_maximum_fusion
  268.6 18.7 %add_convert_fusion = bf16[1,16,128,192]{3,1,2,0:T(8,128)(2,1)S(1)} fusion(bf16[1,16,128,192]{3,1,2,0:T(8,128)(2,1)S(1)} %copy-done.5, bf16[1,16,128,192]{3,1,2,0:T(8,128)(2,1)S(1)} %get-tuple-element.80, bf16[1,16,3,192]{3,1,2,0:T(8,128)(2,1)} %collective-permute-done.2, bf16[1,16,3,192]{3,1,2,0:T(8,128)(2,1)} %collective-permute-done.3, ...), kind=kLoop, calls=%fused_computation.236 | loop fusion | flops 61341696 | bytes 35472128 | tf_op jit(solution)/shard_map/convert_element_type | solution.py:124
  287.3 1.6 copy.47
  288.9 3.3 concatenate.32
  292.3 163.0 %reduce-scatter.4.cloned.1.call-done = bf16[48,192]{1,0:T(8,128)(2,1)} async-done(((bf16[768,192]{1,0:T(8,128)(2,1)}), bf16[48,192]{1,0:T(8,128)(2,1)}) %reduce-scatter.4.cloned.1.call-update) | async-done | bytes 18448 | tf_op jit(solution)/shard_map/reduce_scatter | solution.py:133
  455.4 54.9 %all-reduce.5 = (bf16[12,768]{1,0:T(8,128)(2,1)S(1)}, bf16[48,192]{1,0:T(8,128)(2,1)S(1)}) all-reduce(bf16[12,768]{1,0:T(8,128)(2,1)S(1)} %constant_dynamic-slice_fusion, bf16[48,192]{1,0:T(8,128)(2,1)} %reduce-scatter.4.cloned.1.call-done), channel_id=1, replica_groups=mesh['dp'=16,'lon'=16] {'lon'}, use_global_device_ids=true, to_apply=%region_4.5 | all-reduce | flops 18432 | bytes 73728 | tf_op jit(solution)/shard_map/psum | solution.py:126
  (151 shorter events, 13.8 us)
Async XLA Ops:
  7.2 40.6 %copy-start = (bf16[192,768]{1,0:T(8,128)(2,1)S(1)}, bf16[192,768]{1,0:T(8,128)(2,1)}, u32[]{:S(2)}) copy-start(bf16[192,768]{1,0:T(8,128)(2,1)} %param.13) | copy-start | bytes 884740
  7.2 448.2 %reduce-scatter.4.cloned.1.call-start = ((), (), s32[]{:S(2)}) async-start(), calls=%async_computation.1 | async-start | bytes 417792 | tf_op jit(solution)/shard_map/reduce_scatter | solution.py:133
  14.1 8.9 %copy-start.4 = (bf16[1,16,128,192]{3,1,2,0:T(8,128)(2,1)}, bf16[1,16,128,192]{3,1,2,0:T(8,128)(2,1)S(1)}, u32[]{:S(2)}) copy-start(bf16[1,16,128,192]{3,1,2,0:T(8,128)(2,1)S(1)} %get-tuple-element.136) | copy-start | bytes 2359300
  14.2 9.8 %copy-start.2 = (bf16[1,16,128,192]{3,1,2,0:T(8,128)(2,1)}, bf16[1,16,128,192]{3,1,2,0:T(8,128)(2,1)S(1)}, u32[]{:S(2)}) copy-start(bf16[1,16,128,192]{3,1,2,0:T(8,128)(2,1)S(1)} %get-tuple-element.137) | copy-start | bytes 2359300
  14.2 7.6 %copy-start.54 = (u32[256]{0:T(256)S(1)}, u32[256]{0:T(256)}, u32[]{:S(2)}) copy-start(u32[256]{0:T(256)} %constant.40) | copy-start | bytes 3076
  14.2 8.8 %collective-permute-start.1 = (bf16[1,16,3,192]{3,1,2,0:T(8,128)(2,1)S(1)}, bf16[1,16,3,192]{3,1,2,0:T(8,128)(2,1)S(1)}, u32[]{:S(2)}, u32[]{:S(2)}) collective-permute-start(bf16[1,16,3,192]{3,1,2,0:T(8,128)(2,1)S(1)} %get-tuple-element.86), channel_id=1, source_target_pairs={{1,0},{2,1},{3,2},{4,3},{5,4},{6,5},{7,6},{8,7},{9,8},{10,9},{11,1... | collective-permute-start | bytes 55304 | tf_op jit(solution)/shard_map/ppermute | solution.py:17
  17.5 5.5 %collective-permute-start = (bf16[1,16,3,192]{3,1,2,0:T(8,128)(2,1)S(1)}, bf16[1,16,3,192]{3,1,2,0:T(8,128)(2,1)S(1)}, u32[]{:S(2)}, u32[]{:S(2)}) collective-permute-start(bf16[1,16,3,192]{3,1,2,0:T(8,128)(2,1)S(1)} %get-tuple-element.85), channel_id=1, source_target_pairs={{0,1},{1,2},{2,3},{3,4},{4,5},{5,6},{6,7},{7,8},{8,9},{9,10},{10,1... | collective-permute-start | bytes 55304 | tf_op jit(solution)/shard_map/ppermute | solution.py:16
  17.5 6.4 %copy-start.16 = (f32[1,1,192]{2,1,0:T(1,128)}, f32[1,1,192]{2,1,0:T(1,128)S(1)}, u32[]{:S(2)}) copy-start(f32[1,1,192]{2,1,0:T(1,128)S(1)} %get-tuple-element.87) | copy-start | bytes 2308
  17.5 6.4 %copy-start.17 = (f32[1,1,192]{2,1,0:T(1,128)}, f32[1,1,192]{2,1,0:T(1,128)S(1)}, u32[]{:S(2)}) copy-start(f32[1,1,192]{2,1,0:T(1,128)S(1)} %get-tuple-element.88) | copy-start | bytes 2308
  17.6 6.4 %copy-start.18 = (f32[1,1,192]{2,1,0:T(1,128)}, f32[1,1,192]{2,1,0:T(1,128)S(1)}, u32[]{:S(2)}) copy-start(f32[1,1,192]{2,1,0:T(1,128)S(1)} %get-tuple-element.89) | copy-start | bytes 2308
  17.6 6.4 %copy-start.19 = (f32[1,1,192]{2,1,0:T(1,128)}, f32[1,1,192]{2,1,0:T(1,128)S(1)}, u32[]{:S(2)}) copy-start(f32[1,1,192]{2,1,0:T(1,128)S(1)} %get-tuple-element.90) | copy-start | bytes 2308
  17.6 6.4 %copy-start.20 = (f32[1,1,192]{2,1,0:T(1,128)}, f32[1,1,192]{2,1,0:T(1,128)S(1)}, u32[]{:S(2)}) copy-start(f32[1,1,192]{2,1,0:T(1,128)S(1)} %get-tuple-element.91) | copy-start | bytes 2308
  17.6 6.4 %copy-start.21 = (f32[1,1,192]{2,1,0:T(1,128)}, f32[1,1,192]{2,1,0:T(1,128)S(1)}, u32[]{:S(2)}) copy-start(f32[1,1,192]{2,1,0:T(1,128)S(1)} %get-tuple-element.92) | copy-start | bytes 2308
  17.6 6.4 %copy-start.22 = (f32[1,1,192]{2,1,0:T(1,128)}, f32[1,1,192]{2,1,0:T(1,128)S(1)}, u32[]{:S(2)}) copy-start(f32[1,1,192]{2,1,0:T(1,128)S(1)} %get-tuple-element.93) | copy-start | bytes 2308
  17.6 6.4 %copy-start.23 = (f32[1,1,192]{2,1,0:T(1,128)}, f32[1,1,192]{2,1,0:T(1,128)S(1)}, u32[]{:S(2)}) copy-start(f32[1,1,192]{2,1,0:T(1,128)S(1)} %get-tuple-element.94) | copy-start | bytes 2308
  17.6 6.4 %copy-start.24 = (f32[1,1,192]{2,1,0:T(1,128)}, f32[1,1,192]{2,1,0:T(1,128)S(1)}, u32[]{:S(2)}) copy-start(f32[1,1,192]{2,1,0:T(1,128)S(1)} %get-tuple-element.95) | copy-start | bytes 2308
  17.6 6.4 %copy-start.25 = (f32[1,1,192]{2,1,0:T(1,128)}, f32[1,1,192]{2,1,0:T(1,128)S(1)}, u32[]{:S(2)}) copy-start(f32[1,1,192]{2,1,0:T(1,128)S(1)} %get-tuple-element.96) | copy-start | bytes 2308
  17.6 6.4 %copy-start.26 = (f32[1,1,192]{2,1,0:T(1,128)}, f32[1,1,192]{2,1,0:T(1,128)S(1)}, u32[]{:S(2)}) copy-start(f32[1,1,192]{2,1,0:T(1,128)S(1)} %get-tuple-element.97) | copy-start | bytes 2308
  17.6 6.4 %copy-start.27 = (f32[1,1,192]{2,1,0:T(1,128)}, f32[1,1,192]{2,1,0:T(1,128)S(1)}, u32[]{:S(2)}) copy-start(f32[1,1,192]{2,1,0:T(1,128)S(1)} %get-tuple-element.98) | copy-start | bytes 2308
  17.7 6.4 %copy-start.28 = (f32[1,1,192]{2,1,0:T(1,128)}, f32[1,1,192]{2,1,0:T(1,128)S(1)}, u32[]{:S(2)}) copy-start(f32[1,1,192]{2,1,0:T(1,128)S(1)} %get-tuple-element.99) | copy-start | bytes 2308
  17.7 6.4 %copy-start.29 = (f32[1,1,192]{2,1,0:T(1,128)}, f32[1,1,192]{2,1,0:T(1,128)S(1)}, u32[]{:S(2)}) copy-start(f32[1,1,192]{2,1,0:T(1,128)S(1)} %get-tuple-element.100) | copy-start | bytes 2308
  17.7 6.4 %copy-start.30 = (f32[1,1,192]{2,1,0:T(1,128)}, f32[1,1,192]{2,1,0:T(1,128)S(1)}, u32[]{:S(2)}) copy-start(f32[1,1,192]{2,1,0:T(1,128)S(1)} %get-tuple-element.101) | copy-start | bytes 2308
  17.7 6.4 %copy-start.31 = (f32[1,1,192]{2,1,0:T(1,128)}, f32[1,1,192]{2,1,0:T(1,128)S(1)}, u32[]{:S(2)}) copy-start(f32[1,1,192]{2,1,0:T(1,128)S(1)} %get-tuple-element.102) | copy-start | bytes 2308
  17.7 6.4 %copy-start.32 = (f32[1,1,192]{2,1,0:T(1,128)}, f32[1,1,192]{2,1,0:T(1,128)S(1)}, u32[]{:S(2)}) copy-start(f32[1,1,192]{2,1,0:T(1,128)S(1)} %get-tuple-element.103) | copy-start | bytes 2308
  17.7 6.4 %copy-start.33 = (f32[1,1,192]{2,1,0:T(1,128)}, f32[1,1,192]{2,1,0:T(1,128)S(1)}, u32[]{:S(2)}) copy-start(f32[1,1,192]{2,1,0:T(1,128)S(1)} %get-tuple-element.104) | copy-start | bytes 2308
  17.7 6.4 %copy-start.34 = (f32[1,1,192]{2,1,0:T(1,128)}, f32[1,1,192]{2,1,0:T(1,128)S(1)}, u32[]{:S(2)}) copy-start(f32[1,1,192]{2,1,0:T(1,128)S(1)} %get-tuple-element.105) | copy-start | bytes 2308
  18.3 5.8 %copy-start.39 = (f32[1,1,192]{2,1,0:T(1,128)}, f32[1,1,192]{2,1,0:T(1,128)S(1)}, u32[]{:S(2)}) copy-start(f32[1,1,192]{2,1,0:T(1,128)S(1)} %get-tuple-element.110) | copy-start | bytes 2308
  18.4 5.8 %copy-start.40 = (f32[1,1,192]{2,1,0:T(1,128)}, f32[1,1,192]{2,1,0:T(1,128)S(1)}, u32[]{:S(2)}) copy-start(f32[1,1,192]{2,1,0:T(1,128)S(1)} %get-tuple-element.111) | copy-start | bytes 2308
  18.4 5.8 %copy-start.41 = (f32[1,1,192]{2,1,0:T(1,128)}, f32[1,1,192]{2,1,0:T(1,128)S(1)}, u32[]{:S(2)}) copy-start(f32[1,1,192]{2,1,0:T(1,128)S(1)} %get-tuple-element.112) | copy-start | bytes 2308
  18.4 5.8 %copy-start.42 = (f32[1,1,192]{2,1,0:T(1,128)}, f32[1,1,192]{2,1,0:T(1,128)S(1)}, u32[]{:S(2)}) copy-start(f32[1,1,192]{2,1,0:T(1,128)S(1)} %get-tuple-element.113) | copy-start | bytes 2308
  18.4 5.8 %copy-start.43 = (f32[1,1,192]{2,1,0:T(1,128)}, f32[1,1,192]{2,1,0:T(1,128)S(1)}, u32[]{:S(2)}) copy-start(f32[1,1,192]{2,1,0:T(1,128)S(1)} %get-tuple-element.114) | copy-start | bytes 2308
  18.4 5.8 %copy-start.44 = (f32[1,1,192]{2,1,0:T(1,128)}, f32[1,1,192]{2,1,0:T(1,128)S(1)}, u32[]{:S(2)}) copy-start(f32[1,1,192]{2,1,0:T(1,128)S(1)} %get-tuple-element.115) | copy-start | bytes 2308
  18.4 5.8 %copy-start.45 = (f32[1,1,192]{2,1,0:T(1,128)}, f32[1,1,192]{2,1,0:T(1,128)S(1)}, u32[]{:S(2)}) copy-start(f32[1,1,192]{2,1,0:T(1,128)S(1)} %get-tuple-element.116) | copy-start | bytes 2308
  18.4 5.8 %copy-start.46 = (f32[1,1,192]{2,1,0:T(1,128)}, f32[1,1,192]{2,1,0:T(1,128)S(1)}, u32[]{:S(2)}) copy-start(f32[1,1,192]{2,1,0:T(1,128)S(1)} %get-tuple-element.117) | copy-start | bytes 2308
  18.4 5.8 %copy-start.47 = (f32[1,1,192]{2,1,0:T(1,128)}, f32[1,1,192]{2,1,0:T(1,128)S(1)}, u32[]{:S(2)}) copy-start(f32[1,1,192]{2,1,0:T(1,128)S(1)} %get-tuple-element.118) | copy-start | bytes 2308
  18.4 5.8 %copy-start.48 = (f32[1,1,192]{2,1,0:T(1,128)}, f32[1,1,192]{2,1,0:T(1,128)S(1)}, u32[]{:S(2)}) copy-start(f32[1,1,192]{2,1,0:T(1,128)S(1)} %get-tuple-element.119) | copy-start | bytes 2308
  18.4 5.8 %copy-start.49 = (f32[1,1,192]{2,1,0:T(1,128)}, f32[1,1,192]{2,1,0:T(1,128)S(1)}, u32[]{:S(2)}) copy-start(f32[1,1,192]{2,1,0:T(1,128)S(1)} %get-tuple-element.120) | copy-start | bytes 2308
  18.5 5.8 %copy-start.50 = (f32[1,1,192]{2,1,0:T(1,128)}, f32[1,1,192]{2,1,0:T(1,128)S(1)}, u32[]{:S(2)}) copy-start(f32[1,1,192]{2,1,0:T(1,128)S(1)} %get-tuple-element.121) | copy-start | bytes 2308
  101.5 187.4 %collective-permute-start.6 = (bf16[16,768]{1,0:T(8,128)(2,1)}, bf16[16,768]{1,0:T(8,128)(2,1)}, u32[]{:S(2)}, u32[]{:S(2)}) collective-permute-start(bf16[16,768]{1,0:T(8,128)(2,1)} %fusion), channel_id=1, source_target_pairs={{0,48},{16,64},{32,80},{48,96},{64,112},{80,128},{96,144},{112,160... | collective-permute-start | bytes 73736
  103.4 185.5 %collective-permute-start.5 = (bf16[16,768]{1,0:T(8,128)(2,1)}, bf16[16,768]{1,0:T(8,128)(2,1)}, u32[]{:S(2)}, u32[]{:S(2)}) collective-permute-start(bf16[16,768]{1,0:T(8,128)(2,1)} %fusion), channel_id=1, source_target_pairs={{0,32},{16,48},{32,64},{48,80},{64,96},{80,112},{96,128},{112,144}... | collective-permute-start | bytes 73736
  105.3 183.7 %collective-permute-start.4 = (bf16[16,768]{1,0:T(8,128)(2,1)}, bf16[16,768]{1,0:T(8,128)(2,1)}, u32[]{:S(2)}, u32[]{:S(2)}) collective-permute-start(bf16[16,768]{1,0:T(8,128)(2,1)} %fusion), channel_id=1, source_target_pairs={{0,16},{16,32},{32,48},{48,64},{64,80},{80,96},{96,112},{112,128},... | collective-permute-start | bytes 73736
  135.3 7.3 %copy-start.8 = (f32[24,8,16,128]{3,1,2,0:T(8,128)S(1)}, f32[24,8,16,128]{3,1,2,0:T(8,128)}, u32[]{:S(2)}) copy-start(f32[24,8,16,128]{3,1,2,0:T(8,128)} %convolution_bitcast_fusion) | copy-start | bytes 4718596
  144.2 20.5 %copy-start.3 = (bf16[1,16,128,192]{3,1,2,0:T(8,128)(2,1)S(1)}, bf16[1,16,128,192]{3,1,2,0:T(8,128)(2,1)}, u32[]{:S(2)}) copy-start(bf16[1,16,128,192]{3,1,2,0:T(8,128)(2,1)} %copy-done.2) | copy-start | bytes 2359300
  147.4 109.5 %copy-start.7 = (bf16[1,16,128,192]{3,1,2,0:T(8,128)(2,1)S(1)}, bf16[1,16,128,192]{3,1,2,0:T(8,128)(2,1)}, u32[]{:S(2)}) copy-start(bf16[1,16,128,192]{3,1,2,0:T(8,128)(2,1)} %copy-done.6) | copy-start | bytes 2359300
  147.4 114.4 %collective-permute-start.2 = (bf16[1,16,3,192]{3,1,2,0:T(8,128)(2,1)}, bf16[1,16,3,192]{3,1,2,0:T(8,128)(2,1)}, u32[]{:S(2)}, u32[]{:S(2)}) collective-permute-start(bf16[1,16,3,192]{3,1,2,0:T(8,128)(2,1)} %get-tuple-element.84), channel_id=1, source_target_pairs={{0,1},{1,2},{2,3},{3,4},{4,5},{5,6},{6,7},{7,8},{8,9},{9,10},{10,1... | collective-permute-start | bytes 55304 | tf_op jit(solution)/shard_map/ppermute | solution.py:16
  155.0 111.9 %collective-permute-start.3 = (bf16[1,16,3,192]{3,1,2,0:T(8,128)(2,1)}, bf16[1,16,3,192]{3,1,2,0:T(8,128)(2,1)}, u32[]{:S(2)}, u32[]{:S(2)}) collective-permute-start(bf16[1,16,3,192]{3,1,2,0:T(8,128)(2,1)} %get-tuple-element.83), channel_id=1, source_target_pairs={{1,0},{2,1},{3,2},{4,3},{5,4},{6,5},{7,6},{8,7},{9,8},{10,9},{11,1... | collective-permute-start | bytes 55304 | tf_op jit(solution)/shard_map/ppermute | solution.py:17
  260.1 8.5 %copy-start.5 = (bf16[1,16,128,192]{3,1,2,0:T(8,128)(2,1)S(1)}, bf16[1,16,128,192]{3,1,2,0:T(8,128)(2,1)}, u32[]{:S(2)}) copy-start(bf16[1,16,128,192]{3,1,2,0:T(8,128)(2,1)} %copy-done.4) | copy-start | bytes 2359300
  261.8 27.1 %collective-permute-start.7 = (bf16[12,768]{1,0:T(8,128)(2,1)S(1)}, bf16[12,768]{1,0:T(8,128)(2,1)S(1)}, u32[]{:S(2)}, u32[]{:S(2)}) collective-permute-start(bf16[12,768]{1,0:T(8,128)(2,1)S(1)} %slice.826), channel_id=1, source_target_pairs={{0,64},{16,80},{32,96},{48,112},{64,128},{80,144},{96,160},{112,17... | collective-permute-start | bytes 55304
  (17 other events, 67.4 us)
Sparse Core Ops, SparseCore 0:
  261.9 193.4 reduce-scatter.3
where the time goes:
time: 522 us; the launch traced here: 518 us
  blocking collectives  176 us (34%)
  waiting for transfers between devices  163 us (31%)
  other arithmetic  77.9 us (15%)
  local copies, waits for them, and re-layouts  43.3 us (8%)
  starting transfers between devices  23.6 us (5%)
  matrix products  18.8 us (4%)
  between operations  15.6 us (3%)
    reduce_scatter x1, waiting for transfers between devices, per_device(): lax.psum_scatter(summed_out.astype(jnp.bfloat16), 'dp', scatter_dimension...  163 us
    psum x1, blocking collectives, per_device(): lax.psum((part_kernel, part_gain, part_bias), ('dp', 'lon'))  80.1 us
    psum x1, blocking collectives, per_device(): lax.psum(part_in.astype(jnp.bfloat16), 'lon').astype(jnp.float32)  54.9 us
    unnamed x1, blocking collectives  41.1 us
    reduce_sum x4, other arithmetic, kernel_terms(): cols_out.append(jnp.sum(window * d_float, axis=(0, 1, 2)))  25 us
    unnamed x128, local copies, waits for them, and re-layouts  23 us
    reduce_sum x1, other arithmetic, per_device(): mean_c = jnp.mean(conv, axis=-1, keepdims=True)  19.4 us
    convert_element_type x1, other arithmetic, per_device(): (grad_m.astype(jnp.float32) + mask_f * spread).astype(jnp.bfloat16)  18.7 us
  transfers between devices with their start and end apart: 9, of which 1 were waited for; matrix products, arithmetic and copies ran while one was open for 18% of the time, Pallas kernels for 0%

commit v1 on v0

v1 whole, which is shorter than its diff:
```python
import functools
import math

import jax
import jax.numpy as jnp
from jax import lax
from jax.experimental import pallas as pl
from jax.experimental.pallas import tpu as pltpu
from jax.sharding import PartitionSpec as P

F32 = jnp.float32
BF16 = jnp.bfloat16
MESH = pl.DeviceIdType.MESH
ROWS = 16
CH = 192
HID = 768
LANES = 128
TILES = CH // 8
PEERS = 16
VMEM_BYTES = 60 * 1024 * 1024


def lane_ids(shape):
    return lax.broadcasted_iota(jnp.int32, shape, 1)


def pack_edges(row_of):
    group = ((lane_ids((CH, LANES)) + 4) // 8) % ROWS
    packed = jnp.zeros((CH, LANES), F32)
    for i in range(ROWS):
        row = row_of(i)
        if i:
            row = pltpu.roll(row, 8 * i, axis=1)
        packed = jnp.where(group == i, row, packed)
    return packed


def merge_edges(from_left, from_right):
    low = lane_ids((CH, LANES)) % 8 < 4
    return jnp.where(low, from_right.astype(F32), from_left.astype(F32))


def spread_edges(edges, halo_ref):
    for i in range(ROWS):
        halo_ref[i] = pltpu.roll(edges, (LANES - 8 * i) % LANES, axis=1) if i else edges


def shifted_rows(src, halo, c0, shift):
    lane = lane_ids((8, LANES))
    rows = []
    for r in range(ROWS):
        row = src[r, pl.ds(c0, 8), :]
        if shift > 0:
            row = jnp.where(lane < shift, halo[r, pl.ds(c0, 8), :], row)
        elif shift < 0:
            row = jnp.where(lane >= LANES + shift, halo[r, pl.ds(c0, 8), :], row)
        if shift:
            row = pltpu.roll(row, (LANES - shift) % LANES, axis=1)
        rows.append(row)
    return rows


def conv_tile(src, halo, taps, dst, tile, sign):
    c0 = pl.multiple_of(tile * 8, 8)
    weights = taps[pl.ds(c0, 8), :]
    total = [None] * ROWS
    for b in range(7):
        rows = shifted_rows(src, halo, c0, sign * (b - 3))
        for a in range(7):
            col = 8 * a + b
            w = jnp.broadcast_to(weights[:, col : col + 1], (8, LANES))
            for i in range(ROWS):
                r = i + sign * (a - 3)
                if 0 <= r < ROWS:
                    term = w * rows[r]
                    total[i] = term if total[i] is None else total[i] + term
    for i in range(ROWS):
        dst[i, pl.ds(c0, 8), :] = total[i]


def kernel_grad_tile(src, halo, grad, dst, tile):
    c0 = pl.multiple_of(tile * 8, 8)
    lane = lane_ids((8, LANES))
    out = jnp.zeros((8, LANES), F32)
    for b in range(7):
        rows = shifted_rows(src, halo, c0, b - 3)
        sums = [None] * 7
        for i in range(ROWS):
            g = grad[i, pl.ds(c0, 8), :]
            for a in range(7):
                r = i + a - 3
                if 0 <= r < ROWS:
                    term = g * rows[r]
                    sums[a] = term if sums[a] is None else sums[a] + term
        for a in range(7):
            col = jnp.sum(sums[a], axis=1, keepdims=True)
            out = jnp.where(lane == 8 * a + b, col, out)
    dst[pl.ds(c0, 8), :] = out


def load_taps(kern_ref, stage, taps):
    stage[...] = jnp.zeros_like(stage)
    for a in range(7):
        stage[8 * a : 8 * a + 7, :] = kern_ref[a]
    taps[...] = jnp.transpose(stage[...])


def ring_neighbours():
    me = lax.axis_index("lon")
    return lax.rem(me + PEERS - 1, PEERS), lax.rem(me + 1, PEERS)


def lon_device(lon):
    return (lax.axis_index("dp"), lon)


def edge_kernel(fields, mask, edges, mine, slots, send, recv):
    left, right = ring_neighbours()
    barrier = pltpu.get_barrier_semaphore()
    for peer in (left, right):
        pl.semaphore_signal(barrier, inc=1, device_id=lon_device(peer), device_id_type=MESH)
    maskf = mask[...].astype(F32)
    packed = pack_edges(lambda i: fields[i].astype(F32) * maskf[i : i + 1, :])
    mine[...] = packed.astype(BF16)
    pl.semaphore_wait(barrier, 2)
    copies = []
    for k, peer in enumerate((left, right)):
        copy = pltpu.make_async_remote_copy(
            src_ref=mine,
            dst_ref=slots.at[k],
            send_sem=send.at[k],
            recv_sem=recv.at[k],
            device_id=lon_device(peer),
            device_id_type=MESH,
        )
        copy.start()
        copies.append(copy)
    for copy in copies:
        copy.wait()
    edges[...] = merge_edges(slots[1], slots[0]).astype(BF16)


def gelu_terms(z):
    half = 0.5 * (1.0 + lax.erf(z * (1.0 / math.sqrt(2.0))))
    slope = half + z * (jnp.exp(z * z * -0.5) * (1.0 / math.sqrt(2.0 * math.pi)))
    return z * half, slope


def block_kernel(
    fields, cot, mask, edges, kern, gain_row, w_in, bias_row, w_out_t,
    out, d_conv, d_edges, parts,
    masked, halo, conv, stage, taps, m3, gain_col, bias_col, w_in_t, w_out, aug,
    part_in, part_out, gain_sum, blocks,
):
    maskf = mask[...].astype(F32)
    for i in range(ROWS):
        m3[i] = maskf[i : i + 1, :]
        masked[i] = fields[i].astype(F32) * maskf[i : i + 1, :]
    spread_edges(edges[...].astype(F32), halo)
    load_taps(kern, stage, taps)
    gain_col[...] = jnp.transpose(jnp.broadcast_to(gain_row[...], (LANES, CH)))
    bias_col[...] = jnp.transpose(jnp.broadcast_to(bias_row[...], (LANES, HID)))
    w_in_t[...] = jnp.transpose(w_in[...].astype(F32)).astype(BF16)
    w_out[...] = jnp.transpose(w_out_t[...].astype(F32)).astype(BF16)
    part_in[...] = jnp.zeros_like(part_in)
    part_out[...] = jnp.zeros_like(part_out)
    gain_sum[...] = jnp.zeros_like(gain_sum)
    first = lax.broadcasted_iota(jnp.int32, (16, 2 * LANES), 0) == 0
    aug[CH : CH + 16, :] = jnp.where(first, 1.0, 0.0).astype(BF16)

    def conv_step(tile, carry):
        conv_tile(masked, halo, taps, conv, tile, 1)
        return carry

    lax.fori_loop(0, TILES, conv_step, 0)

    def pair(ref, k):
        return jnp.concatenate(
            [ref[2 * k].astype(F32), ref[2 * k + 1].astype(F32)], axis=1
        )

    def chunk(k, carry):
        c = pair(conv, k)
        mu = jnp.sum(c, axis=0, keepdims=True) * (1.0 / CH)
        centered = c - mu
        var = jnp.sum(centered * centered, axis=0, keepdims=True) * (1.0 / CH)
        inv = lax.rsqrt(var + 1e-6)
        nhat = centered * inv
        gain2 = jnp.concatenate([gain_col[...], gain_col[...]], axis=1)
        aug[0:CH, :] = (nhat * gain2).astype(BF16)
        m2 = pair(m3, k)
        gm = (pair(cot, k) * m2).astype(BF16)
        branch = jnp.zeros((CH, 2 * LANES), F32)
        d_normed = jnp.zeros((CH, 2 * LANES), F32)
        for h in range(3):
            hs = slice(256 * h, 256 * h + 256)
            bias2 = jnp.concatenate([bias_col[hs, :], bias_col[hs, :]], axis=1)
            pre = jnp.dot(w_in_t[hs, :], aug[0:CH, :], preferred_element_type=F32) + bias2
            d_act = jnp.dot(w_out[hs, :], gm, preferred_element_type=F32)
            act, slope = gelu_terms(pre)
            act = act.astype(BF16)
            d_pre = (d_act * slope).astype(BF16)
            branch = branch + jnp.dot(w_out_t[:, hs], act, preferred_element_type=F32)
            d_normed = d_normed + jnp.dot(w_in[:, hs], d_pre, preferred_element_type=F32)
            part_in[:, hs] += lax.dot_general(
                aug[...], d_pre, (((1,), (1,)), ((), ())), preferred_element_type=F32
            )
            part_out[hs, :] += lax.dot_general(
                act, gm, (((1,), (1,)), ((), ())), preferred_element_type=F32
            )
        result = (m2 * (pair(fields, k) + branch)).astype(BF16)
        out[2 * k] = result[:, :LANES]
        out[2 * k + 1] = result[:, LANES:]
        along = d_normed * nhat
        gain_sum[...] += along[:, :LANES] + along[:, LANES:]
        d_hat = d_normed * gain2
        mean_d = jnp.sum(d_hat, axis=0, keepdims=True) * (1.0 / CH)
        mean_dn = jnp.sum(d_hat * nhat, axis=0, keepdims=True) * (1.0 / CH)
        d = (inv * (d_hat - mean_d - nhat * mean_dn)).astype(BF16)
        d_conv[2 * k] = d[:, :LANES]
        d_conv[2 * k + 1] = d[:, LANES:]
        return carry

    lax.fori_loop(0, ROWS // 2, chunk, 0)

    d_edges[...] = pack_edges(lambda i: d_conv[i].astype(F32)).astype(BF16)
    gain_total = jnp.sum(jnp.transpose(gain_sum[...]), axis=0, keepdims=True)
    blocks[...] = jnp.zeros_like(blocks)
    for d in range(PEERS):
        for g in range(3):
            lanes = slice(256 * g, 256 * g + 256)
            blocks[16 * g : 16 * g + 12, :] = part_in[12 * d : 12 * d + 12, lanes]
            blocks[16 * g + 12 : 16 * g + 13, :] = part_in[CH : CH + 1, lanes]
        blocks[13:14, 0:CH] = gain_total
        parts[0, d] = blocks[...].astype(BF16)
    for d in range(PEERS):
        parts[1, d, :, 0:CH] = part_out[48 * d : 48 * d + 48, :].astype(BF16)
        parts[1, d, :, CH:256] = jnp.zeros((48, 64), BF16)


def grad_kernel(
    fields, cot, mask, edges, kern, d_conv, d_edges, parts,
    grad_fields, g_in, g_out, g_gain, g_bias, g_kern,
    masked, m_halo, grad, d_halo, spread, stage, taps, taps_grad, small,
    d_slots, sib_in, half_sum, dp_in, dp_sum, lon_in, total, sib_total,
    k_pieces, k_lon, k_sum, k_dp, k_full, k_all,
    nb_send, nb_recv, one_send, one_recv, dp_send, dp_recv, lon_send, lon_recv,
    ks_send, ks_recv, kd_send, kd_recv, kg_send, kg_recv,
    *, scale
):
    dp, lon = lax.axis_index("dp"), lax.axis_index("lon")
    left, right = ring_neighbours()
    core = lax.rem(lon, 2)
    sibling = lon + 1 - 2 * core
    barrier = pltpu.get_barrier_semaphore()

    def dp_peer(k):
        return (lax.rem(dp + k, PEERS), lon)

    def lon_peer(k):
        return (dp, lax.rem(lon + k, PEERS))

    def greet(k, carry):
        pl.semaphore_signal(barrier, inc=1, device_id=dp_peer(k), device_id_type=MESH)
        pl.semaphore_signal(barrier, inc=1, device_id=lon_peer(k), device_id_type=MESH)
        return carry

    lax.fori_loop(1, PEERS, greet, 0)

    def remote(src, dst, send, recv, device):
        return pltpu.make_async_remote_copy(
            src_ref=src, dst_ref=dst, send_sem=send, recv_sem=recv,
            device_id=device, device_id_type=MESH,
        )

    def to_sibling():
        return remote(
            parts.at[1 - core], sib_in, one_send.at[0], one_recv.at[0], lon_device(sibling)
        )

    def to_neighbour(k):
        peer = (left, right)[k]
        return remote(d_edges, d_slots.at[k], nb_send.at[k], nb_recv.at[k], lon_device(peer))

    def over_dp(k):
        return remote(
            half_sum.at[lax.rem(dp + k, PEERS)], dp_in.at[k], dp_send.at[k], dp_recv.at[k],
            dp_peer(k),
        )

    def over_lon(k):
        return remote(dp_sum, lon_in.at[k], lon_send.at[k], lon_recv.at[k], lon_peer(2 * k))

    def last_sibling():
        return remote(total, sib_total, one_send.at[1], one_recv.at[1], lon_device(sibling))

    def kernel_scatter(k):
        return remote(
            k_pieces.at[lax.rem(lon + k, PEERS)], k_lon.at[k], ks_send.at[k], ks_recv.at[k],
            lon_peer(k),
        )

    def kernel_over_dp(k):
        return remote(k_sum, k_dp.at[k], kd_send.at[k], kd_recv.at[k], dp_peer(k))

    def kernel_gather(k):
        return remote(k_full, k_all.at[k], kg_send.at[k], kg_recv.at[k], lon_peer(k))

    def start_all(make, count):
        def body(k, carry):
            make(k).start()
            return carry

        lax.fori_loop(1, count, body, 0)

    def wait_all(make, count):
        def body(k, carry):
            make(k).wait()
            return carry

        lax.fori_loop(1, count, body, 0)

    def sum_slots(own, slots, count):
        def body(k, acc):
            return acc + slots[k].astype(F32)

        return lax.fori_loop(1, count, body, own.astype(F32))

    def tiles(step, lo, hi):
        def body(t, carry):
            step(t)
            return carry

        lax.fori_loop(lo, hi, body, 0)

    pl.semaphore_wait(barrier, 2 * (PEERS - 1))
    for k in range(2):
        to_neighbour(k).start()
    to_sibling().start()

    maskf = mask[...].astype(F32)
    for i in range(ROWS):
        masked[i] = fields[i].astype(F32) * maskf[i : i + 1, :]
        grad[i] = d_conv[i].astype(F32)
    spread_edges(edges[...].astype(F32), m_halo)
    load_taps(kern, stage, taps)

    def kernel_step(t):
        kernel_grad_tile(masked, m_halo, grad, taps_grad, t)

    def spread_step(t):
        conv_tile(grad, d_halo, taps, spread, t, -1)

    tiles(kernel_step, 0, 8)
    to_sibling().wait()

    def add_half(d, carry):
        half_sum[d] = (parts[core, d].astype(F32) + sib_in[d].astype(F32)).astype(BF16)
        return carry

    lax.fori_loop(0, PEERS, add_half, 0)
    start_all(over_dp, PEERS)
    tiles(kernel_step, 8, TILES)

    flipped = jnp.transpose(taps_grad[...])
    for p in range(PEERS):
        k_pieces[p] = flipped[4 * p : 4 * p + 4, :]
    start_all(kernel_scatter, PEERS)

    for k in range(2):
        to_neighbour(k).wait()
    spread_edges(merge_edges(d_slots[1], d_slots[0]), d_halo)
    tiles(spread_step, 0, 8)

    wait_all(kernel_scatter, PEERS)
    k_sum[...] = sum_slots(k_pieces[lon], k_lon, PEERS)
    start_all(kernel_over_dp, PEERS)
    tiles(spread_step, 8, 16)

    wait_all(over_dp, PEERS)
    dp_sum[...] = sum_slots(half_sum[dp], dp_in, PEERS).astype(BF16)
    start_all(over_lon, PEERS // 2)
    wait_all(kernel_over_dp, PEERS)
    k_full[...] = sum_slots(k_sum[...], k_dp, PEERS)
    start_all(kernel_gather, PEERS)
    tiles(spread_step, 16, TILES)

    wait_all(over_lon, PEERS // 2)
    total[...] = sum_slots(dp_sum[...], lon_in, PEERS // 2)
    last_sibling().start()

    for i in range(ROWS):
        m = maskf[i : i + 1, :]
        grad_fields[i] = (m * (cot[i].astype(F32) + spread[i])).astype(BF16)

    wait_all(kernel_gather, PEERS)
    k_all[0] = k_full[...]
    for p in range(PEERS):
        small[4 * p : 4 * p + 4, :] = k_all[lax.rem(lon - p + PEERS, PEERS)]
    for a in range(7):
        g_kern[a] = small[8 * a : 8 * a + 7, :] * scale

    last_sibling().wait()
    mine, other = total[...] * scale, sib_total[...] * scale
    even = core == 0
    first = jnp.where(even, mine, other)
    second = jnp.where(even, other, mine)
    for g in range(3):
        lanes = slice(256 * g, 256 * g + 256)
        g_in[:, lanes] = first[16 * g : 16 * g + 12, :]
        g_bias[:, lanes] = first[16 * g + 12 : 16 * g + 13, :]
    g_gain[...] = first[13:14, 0:CH]
    g_out[...] = second[:, 0:CH]


def vmem():
    return pl.BlockSpec(memory_space=pltpu.VMEM)


def per_device(fields, cotangent, land_sea, kernel, ln_gain, weight_in, bias_in, weight_out):
    x = jnp.transpose(fields, (0, 1, 3, 2)).reshape(ROWS, CH, LANES)
    cot = jnp.transpose(cotangent, (0, 1, 3, 2)).reshape(ROWS, CH, LANES)
    w_out_t = jnp.transpose(weight_out)
    gain_row = ln_gain.reshape(1, CH)
    bias_row = bias_in.reshape(1, HID)
    dma = pltpu.SemaphoreType.DMA
    big = (ROWS, CH, LANES)

    edges = pl.pallas_call(
        edge_kernel,
        name="field_edges",
        out_shape=jax.ShapeDtypeStruct((CH, LANES), BF16),
        in_specs=[vmem()] * 2,
        out_specs=vmem(),
        scratch_shapes=[
            pltpu.VMEM((CH, LANES), BF16),
            pltpu.VMEM((2, CH, LANES), BF16),
            dma((2,)),
            dma((2,)),
        ],
        compiler_params=pltpu.CompilerParams(
            collective_id=0, has_side_effects=True, vmem_limit_bytes=VMEM_BYTES
        ),
    )(x, land_sea)

    out, d_conv, d_edges, parts = pl.pallas_call(
        block_kernel,
        name="block",
        out_shape=(
            jax.ShapeDtypeStruct(big, BF16),
            jax.ShapeDtypeStruct(big, BF16),
            jax.ShapeDtypeStruct((CH, LANES), BF16),
            jax.ShapeDtypeStruct((2, PEERS, 48, 256), BF16),
        ),
        in_specs=[vmem()] * 9,
        out_specs=(vmem(),) * 4,
        scratch_shapes=[
            pltpu.VMEM(big, F32),
            pltpu.VMEM(big, F32),
            pltpu.VMEM(big, F32),
            pltpu.VMEM((LANES, CH), F32),
            pltpu.VMEM((CH, LANES), F32),
            pltpu.VMEM((ROWS, 1, LANES), F32),
            pltpu.VMEM((CH, LANES), F32),
            pltpu.VMEM((HID, LANES), F32),
            pltpu.VMEM((HID, CH), BF16),
            pltpu.VMEM((HID, CH), BF16),
            pltpu.VMEM((CH + 16, 2 * LANES), BF16),
            pltpu.VMEM((CH + 16, HID), F32),
            pltpu.VMEM((HID, CH), F32),
            pltpu.VMEM((CH, LANES), F32),
            pltpu.VMEM((48, 256), F32),
        ],
        compiler_params=pltpu.CompilerParams(vmem_limit_bytes=VMEM_BYTES),
    )(x, cot, land_sea, edges, kernel, gain_row, weight_in, bias_row, w_out_t)

    total_cells = ROWS * LANES * lax.axis_size("dp") * lax.axis_size("lon")
    piece = (4, CH)
    grad_fields, g_in, g_out, g_gain, g_bias, g_kern = pl.pallas_call(
        functools.partial(grad_kernel, scale=1.0 / math.sqrt(total_cells)),
        name="grads",
        out_shape=(
            jax.ShapeDtypeStruct(big, BF16),
            jax.ShapeDtypeStruct((12, HID), F32),
            jax.ShapeDtypeStruct((48, CH), F32),
            jax.ShapeDtypeStruct((1, CH), F32),
            jax.ShapeDtypeStruct((1, HID), F32),
            jax.ShapeDtypeStruct((7, 7, CH), F32),
        ),
        in_specs=[vmem()] * 8,
        out_specs=(vmem(),) * 6,
        scratch_shapes=[
            pltpu.VMEM(big, F32),
            pltpu.VMEM(big, F32),
            pltpu.VMEM(big, F32),
            pltpu.VMEM(big, F32),
            pltpu.VMEM(big, F32),
            pltpu.VMEM((LANES, CH), F32),
            pltpu.VMEM((CH, LANES), F32),
            pltpu.VMEM((CH, LANES), F32),
            pltpu.VMEM((4 * PEERS, CH), F32),
            pltpu.VMEM((2, CH, LANES), BF16),
            pltpu.VMEM((PEERS, 48, 256), BF16),
            pltpu.VMEM((PEERS, 48, 256), BF16),
            pltpu.VMEM((PEERS, 48, 256), BF16),
            pltpu.VMEM((48, 256), BF16),
            pltpu.VMEM((PEERS // 2, 48, 256), BF16),
            pltpu.VMEM((48, 256), F32),
            pltpu.VMEM((48, 256), F32),
            pltpu.VMEM((PEERS,) + piece, F32),
            pltpu.VMEM((PEERS,) + piece, F32),
            pltpu.VMEM(piece, F32),
            pltpu.VMEM((PEERS,) + piece, F32),
            pltpu.VMEM(piece, F32),
            pltpu.VMEM((PEERS,) + piece, F32),
            dma((2,)),
            dma((2,)),
            dma((2,)),
            dma((2,)),
            dma((PEERS,)),
            dma((PEERS,)),
            dma((PEERS // 2,)),
            dma((PEERS // 2,)),
            dma((PEERS,)),
            dma((PEERS,)),
            dma((PEERS,)),
            dma((PEERS,)),
            dma((PEERS,)),
            dma((PEERS,)),
        ],
        compiler_params=pltpu.CompilerParams(
            collective_id=1, has_side_effects=True, vmem_limit_bytes=VMEM_BYTES
        ),
    )(x, cot, land_sea, edges, kernel, d_conv, d_edges, parts)

    def back(y):
        return jnp.transpose(y[None], (0, 1, 3, 2))

    return (
        back(out),
        back(grad_fields),
        g_in,
        g_out,
        g_kern,
        g_gain.reshape(CH),
        g_bias.reshape(HID),
    )


def solution(mesh):
    placed = (
        P("dp", None, "lon", None),
        P("dp", None, "lon", None),
        P(None, "lon"),
        P(),
        P(),
        P(),
        P(),
        P(),
    )
    return jax.shard_map(
        per_device,
        mesh=mesh,
        in_specs=placed,
        out_specs=(
            P("dp", None, "lon", None),
            P("dp", None, "lon", None),
            P("dp", None),
            P("dp", None),
            P(),
            P(),
            P(),
        ),
        check_vma=False,
    )
```

time: 522 us -> 79.5 us (0.15)
  blocking collectives: 176 us -> 0 us
  waiting for transfers between devices: 163 us -> 0 us
  other arithmetic: 77.9 us -> 0.6 us
  Pallas kernels: 0 us -> 71 us
  local copies, waits for them, and re-layouts: 43.3 us -> 6.87 us
  starting transfers between devices: 23.6 us -> 0 us
  matrix products: 18.8 us -> 0 us
  between operations: 15.6 us -> 0.67 us
    reduce_scatter x1 -> x0, waiting for transfers between devices: 163 us -> none  [per_device(): lax.psum_scatter(summed_out.astype(jnp.bfloat16), 'dp', scatter_dimension...]
    psum x2 -> x0, blocking collectives: 135 us -> none  [the longest x1 80.1 us: per_device(): lax.psum((part_kernel, part_gain, part_bias), ('dp', 'lon'))]
    pallas_call x0 -> x3, Pallas kernels: none -> 71 us  [the longest x1 41.3 us: per_device(): pl.pallas_call(functools.partial(grad_kernel, scale=1.0 / math.sqrt(total...]
    reduce_sum x7 -> x0, other arithmetic: 48.3 us -> none  [the longest x4 25 us: kernel_terms(): cols_out.append(jnp.sum(window * d_float, axis=(0, 1, 2)))]
    unnamed x1 -> x0, blocking collectives: 41.1 us -> none
    convert_element_type x4 -> x0, other arithmetic: 22 us -> none  [the longest x1 18.7 us: per_device(): (grad_m.astype(jnp.float32) + mask_f * spread).astype(jnp.bfloat16)]
    dot_general x6 -> x0, matrix products: 18.8 us -> none  [the longest x1 4.63 us: per_device(): lax.dot_general(grad_flat, weight_out, (((1,), (1,)), ((), ())), preferre...]
    unnamed x128 -> x17, local copies, waits for them, and re-layouts: 23 us -> 6.29 us
  transfers between devices with their start and end apart: 9 -> 0, of which waited for: 1 -> 0; matrix products, arithmetic and copies ran while one was open for 18% -> 0% of each run, Pallas kernels for 0% -> 0%
where the time goes in v1:
time: 79.5 us; the launch traced here: 79.1 us
  Pallas kernels  71 us (89%)
  local copies, waits for them, and re-layouts  6.87 us (9%)
    pallas_call x1, Pallas kernels, per_device(): pl.pallas_call(functools.partial(grad_kernel, scale=1.0 / math.sqrt(total...  41.3 us
    pallas_call x1, Pallas kernels, per_device(): pl.pallas_call(block_kernel, name='block', out_shape=(jax.ShapeDtypeStruc...  22.5 us
    pallas_call x1, Pallas kernels, per_device(): pl.pallas_call(edge_kernel, name='field_edges', out_shape=jax.ShapeDtypeS...  7.24 us
    unnamed x17, local copies, waits for them, and re-layouts  6.29 us

profile of v1, /device:TPU:1, one launch (start us, length us, event | category | flops | bytes accessed | tf_op | source)
XLA Modules:
  0.0 79.1 jit_solution(17923754704803741057)
XLA Ops:
  0.6 0.0 copy-start.3
  0.6 0.7 copy-done.3
  1.3 0.6 reshape.35.bias_row
  1.9 7.2 %field_edges.1.edges = bf16[192,128]{1,0:T(8,128)(2,1)} custom-call(bf16[16,192,128]{2,1,0:T(8,128)(2,1)} %bitcast.15, s32[16,128]{1,0:T(8,128)} %mask.5), custom_call_target="tpu_custom_call" | custom-call | tf_op jit(solution)/shard_map/field_edges/pallas_call | solution.py:429
  9.1 22.5 %block.1 = (bf16[16,192,128]{2,1,0:T(8,128)(2,1)}, bf16[16,192,128]{2,1,0:T(8,128)(2,1)}, bf16[192,128]{1,0:T(8,128)(2,1)}, bf16[2,16,48,256]{3,2,1,0:T(8,128)(2,1)}) custom-call(bf16[16,192,128]{2,1,0:T(8,128)(2,1)} %bitcast.16, bf16[16,192,128]{2,1,0:T(8,128)(2,1)} %bitcast.18, s32[16,128]{1,0:T(8,128)} %mask.5, bf16[192,128]{1,0:T(8,128)(2,1)} %field_edges.1.edges, ...), custom_call_target="tpu_custom_call" | custom-call | tf_op jit(solution)/shard_map/block/pallas_call | solution.py:446
  31.6 41.3 %grads.1 = (bf16[16,192,128]{2,1,0:T(8,128)(2,1)}, f32[12,768]{1,0:T(8,128)}, f32[48,192]{1,0:T(8,128)}, f32[1,192]{1,0:T(1,128)}, f32[1,768]{1,0:T(1,128)}, /*index=5*/f32[7,7,192]{2,1,0:T(8,128)}) custom-call(bf16[16,192,128]{2,1,0:T(8,128)(2,1)} %bitcast.17, bf16[16,192,128]{2,1,0:T(8,128)(2,1)} %bitcast.19, s32[16,128]{1,0:T(8,128)} %mask.5, ...), custom_call_target="tpu_custom_call" | custom-call | tf_op jit(solution)/shard_map/grads/pallas_call | solution.py:479
  72.9 0.0 copy-start.4
  72.9 0.7 copy-done.4
  73.6 0.6 reduce
  74.2 0.0 copy-start.2
  74.2 2.1 %copy.20 = bf16[1,16,128,192]{2,3,1,0:T(8,128)(2,1)} copy(bf16[1,16,128,192]{2,3,1,0:T(8,128)(2,1)} %bitcast.20) | data formatting | bytes 1572864
  76.3 0.0 copy-done.2
  76.3 0.0 copy-start.1
  76.3 0.6 copy.21
  76.9 0.2 copy-done.1
  77.1 0.0 copy-start
  77.1 0.6 copy.22
  77.7 0.2 copy-done
  77.9 0.0 copy-start.5
  77.9 0.6 copy.23
  78.5 0.0 copy-done.5
  78.6 0.6 copy.24
Async XLA Ops:
  0.6 0.7 copy-start.3
  72.9 0.7 copy-start.4
  74.2 2.1 %copy-start.2 = (f32[12,768]{1,0:T(8,128)S(1)}, f32[12,768]{1,0:T(8,128)}, u32[]{:S(2)}) copy-start(f32[12,768]{1,0:T(8,128)} %get-tuple-element.36) | copy-start | bytes 110596
  76.3 0.8 %copy-start.1 = (f32[48,192]{1,0:T(8,128)S(1)}, f32[48,192]{1,0:T(8,128)}, u32[]{:S(2)}) copy-start(f32[48,192]{1,0:T(8,128)} %get-tuple-element.37) | copy-start | bytes 110596
  77.1 0.8 %copy-start = (f32[7,7,192]{2,1,0:T(8,128)S(1)}, f32[7,7,192]{2,1,0:T(8,128)}, u32[]{:S(2)}) copy-start(f32[7,7,192]{2,1,0:T(8,128)} %get-tuple-element.38) | copy-start | bytes 112900
  77.9 0.7 copy-start.5

commit v2 on v1

v2 whole, which is shorter than its diff:
```python
import functools
import math

import jax
import jax.numpy as jnp
from jax import lax
from jax.experimental import pallas as pl
from jax.experimental.pallas import tpu as pltpu
from jax.sharding import PartitionSpec as P

F32 = jnp.float32
BF16 = jnp.bfloat16
MESH = pl.DeviceIdType.MESH
ROWS = 16
CH = 192
HID = 768
LANES = 128
TILES = CH // 8
PEERS = 16
VMEM_BYTES = 60 * 1024 * 1024


def lane_ids(shape):
    return lax.broadcasted_iota(jnp.int32, shape, 1)


def pack_edges(row_of):
    group = ((lane_ids((CH, LANES)) + 4) // 8) % ROWS
    packed = jnp.zeros((CH, LANES), F32)
    for i in range(ROWS):
        row = row_of(i)
        if i:
            row = pltpu.roll(row, 8 * i, axis=1)
        packed = jnp.where(group == i, row, packed)
    return packed


def merge_edges(from_left, from_right):
    low = lane_ids((CH, LANES)) % 8 < 4
    return jnp.where(low, from_right.astype(F32), from_left.astype(F32))


def spread_edges(edges, halo_ref):
    for i in range(ROWS):
        halo_ref[i] = pltpu.roll(edges, (LANES - 8 * i) % LANES, axis=1) if i else edges


def shifted_rows(src, halo, c0, shift):
    lane = lane_ids((8, LANES))
    rows = []
    for r in range(ROWS):
        row = src[r, pl.ds(c0, 8), :]
        if shift > 0:
            row = jnp.where(lane < shift, halo[r, pl.ds(c0, 8), :], row)
        elif shift < 0:
            row = jnp.where(lane >= LANES + shift, halo[r, pl.ds(c0, 8), :], row)
        if shift:
            row = pltpu.roll(row, (LANES - shift) % LANES, axis=1)
        rows.append(row)
    return rows


def conv_tile(src, halo, taps, dst, tile, sign):
    c0 = pl.multiple_of(tile * 8, 8)
    weights = taps[pl.ds(c0, 8), :]
    total = [None] * ROWS
    for b in range(7):
        rows = shifted_rows(src, halo, c0, sign * (b - 3))
        for a in range(7):
            col = 8 * a + b
            w = jnp.broadcast_to(weights[:, col : col + 1], (8, LANES))
            for i in range(ROWS):
                r = i + sign * (a - 3)
                if 0 <= r < ROWS:
                    term = w * rows[r]
                    total[i] = term if total[i] is None else total[i] + term
    for i in range(ROWS):
        dst[i // 2, pl.ds(c0, 8), LANES * (i % 2) : LANES * (i % 2) + LANES] = total[i]


def kernel_grad_tile(src, halo, grad, dst, tile):
    c0 = pl.multiple_of(tile * 8, 8)
    lane = lane_ids((8, LANES))
    out = jnp.zeros((8, LANES), F32)
    for b in range(7):
        rows = shifted_rows(src, halo, c0, b - 3)
        sums = [None] * 7
        for i in range(ROWS):
            g = grad[i, pl.ds(c0, 8), :]
            for a in range(7):
                r = i + a - 3
                if 0 <= r < ROWS:
                    term = g * rows[r]
                    sums[a] = term if sums[a] is None else sums[a] + term
        for a in range(7):
            col = jnp.sum(sums[a], axis=1, keepdims=True)
            out = jnp.where(lane == 8 * a + b, col, out)
    dst[pl.ds(c0, 8), :] = out


def load_taps(kern_ref, stage, taps):
    stage[...] = jnp.zeros_like(stage)
    for a in range(7):
        stage[8 * a : 8 * a + 7, :] = kern_ref[a]
    taps[...] = jnp.transpose(stage[...])


def ring_neighbours():
    me = lax.axis_index("lon")
    return lax.rem(me + PEERS - 1, PEERS), lax.rem(me + 1, PEERS)


def lon_device(lon):
    return (lax.axis_index("dp"), lon)


def gelu_terms(z):
    half = 0.5 * (1.0 + lax.erf(z * (1.0 / math.sqrt(2.0))))
    slope = half + z * (jnp.exp(z * z * -0.5) * (1.0 / math.sqrt(2.0 * math.pi)))
    return z * half, slope


def loop(lo, hi, step):
    def body(t, carry):
        step(t)
        return carry

    lax.fori_loop(lo, hi, body, 0)


def half(i):
    return slice(LANES * (i % 2), LANES * (i % 2) + LANES)


def main_kernel(
    fields, cot_hbm, mask, kern, gain_row, w_in_hbm, bias_row, w_out_t_hbm,
    out_hbm, grad_fields, totals, kern_total,
    cot, w_in_raw, w_out_t_raw, out,
    masked, m_halo, grad, d_halo, conv, branch, d_normed,
    stage, taps, taps_grad, m3, gain_col, bias_col,
    w_in_t, w_in, w_out, w_out_t, aug, gm, inv,
    part_in, part_out, gain_sum, block,
    m_edges, m_slots, d_edges, d_slots,
    parts, sib_in, half_sum, dp_in, dp_sum, lon_in, total, sib_total,
    k_pieces, k_lon, k_sum, k_dp, k_full, k_all,
    load_sem, m_send, m_recv, d_send, d_recv, sib_send, sib_recv, last_send, last_recv,
    dp_send, dp_recv, lon_send, lon_recv,
    ks_send, ks_recv, kd_send, kd_recv, kg_send, kg_recv,
):
    dp, lon = lax.axis_index("dp"), lax.axis_index("lon")
    left, right = ring_neighbours()
    core = lax.rem(lon, 2)
    sibling = lon + 1 - 2 * core
    barrier = pltpu.get_barrier_semaphore()

    def dp_peer(k):
        return (lax.rem(dp + k, PEERS), lon)

    def lon_peer(k):
        return (dp, lax.rem(lon + k, PEERS))

    def greet(k):
        pl.semaphore_signal(barrier, inc=1, device_id=dp_peer(k), device_id_type=MESH)
        pl.semaphore_signal(barrier, inc=1, device_id=lon_peer(k), device_id_type=MESH)

    def remote(src, dst, send, recv, device):
        return pltpu.make_async_remote_copy(
            src_ref=src, dst_ref=dst, send_sem=send, recv_sem=recv,
            device_id=device, device_id_type=MESH,
        )

    def field_edge(k):
        peer = (left, right)[k]
        return remote(m_edges, m_slots.at[k], m_send.at[k], m_recv.at[k], lon_device(peer))

    def grad_edge(k):
        peer = (left, right)[k]
        return remote(d_edges, d_slots.at[k], d_send.at[k], d_recv.at[k], lon_device(peer))

    def to_sibling(h):
        return remote(
            parts.at[h, 1 - core], sib_in.at[h], sib_send.at[h], sib_recv.at[h],
            lon_device(sibling),
        )

    def over_dp(h):
        def make(k):
            return remote(
                half_sum.at[h, lax.rem(dp + k, PEERS)], dp_in.at[h, k],
                dp_send.at[h, k], dp_recv.at[h, k], dp_peer(k),
            )

        return make

    def over_lon(k):
        return remote(dp_sum, lon_in.at[k], lon_send.at[k], lon_recv.at[k], lon_peer(2 * k))

    def last_sibling():
        return remote(total, sib_total, last_send, last_recv, lon_device(sibling))

    def kernel_scatter(k):
        return remote(
            k_pieces.at[lax.rem(lon + k, PEERS)], k_lon.at[k], ks_send.at[k], ks_recv.at[k],
            lon_peer(k),
        )

    def kernel_over_dp(k):
        return remote(k_sum, k_dp.at[k], kd_send.at[k], kd_recv.at[k], dp_peer(k))

    def kernel_gather(k):
        return remote(k_full, k_all.at[k], kg_send.at[k], kg_recv.at[k], lon_peer(k))

    def start_all(make, count):
        loop(1, count, lambda k: make(k).start())

    def wait_all(make, count):
        loop(1, count, lambda k: make(k).wait())

    def sum_slots(own, slots, count):
        def body(k, acc):
            return acc + slots[k].astype(F32)

        return lax.fori_loop(1, count, body, own.astype(F32))

    loads = [
        pltpu.make_async_copy(src, dst, load_sem.at[n])
        for n, (src, dst) in enumerate(
            ((w_in_hbm, w_in_raw), (w_out_t_hbm, w_out_t_raw), (cot_hbm, cot))
        )
    ]
    for load in loads:
        load.start()
    loop(1, PEERS, greet)

    maskf = mask[...].astype(F32)
    for i in range(ROWS):
        m3[i] = maskf[i : i + 1, :]
        masked[i] = fields[i].astype(F32) * maskf[i : i + 1, :]
    m_edges[...] = pack_edges(lambda i: masked[i]).astype(BF16)
    pl.semaphore_wait(barrier, 2 * (PEERS - 1))
    for k in range(2):
        field_edge(k).start()

    load_taps(kern, stage, taps)
    gain_col[...] = jnp.transpose(jnp.broadcast_to(gain_row[...], (LANES, CH)))
    bias_wide = jnp.transpose(jnp.broadcast_to(bias_row[...], (LANES, HID)))
    loads[0].wait()
    loads[1].wait()
    in_t = jnp.transpose(w_in_raw[...].astype(F32)).astype(BF16)
    out_n = jnp.transpose(w_out_t_raw[...].astype(F32)).astype(BF16)
    for h in range(3):
        for d in range(PEERS):
            to = slice(16 * d, 16 * d + 16)
            at = slice(48 * d + 16 * h, 48 * d + 16 * h + 16)
            w_in_t[h, to, :] = in_t[at, :]
            w_out[h, to, :] = out_n[at, :]
            bias_col[h, to, :] = bias_wide[at, :]
        w_in[h] = jnp.transpose(w_in_t[h].astype(F32)).astype(BF16)
        w_out_t[h] = jnp.transpose(w_out[h].astype(F32)).astype(BF16)
    ones_row = lax.broadcasted_iota(jnp.int32, (16, 2 * LANES), 0) == 0
    for k in range(ROWS // 2):
        aug[k, CH : CH + 16, :] = jnp.where(ones_row, 1.0, 0.0).astype(BF16)
    gain_sum[...] = jnp.zeros_like(gain_sum)
    block[...] = jnp.zeros_like(block)

    for k in range(2):
        field_edge(k).wait()
    spread_edges(merge_edges(m_slots[1], m_slots[0]), m_halo)
    loop(0, TILES, lambda t: conv_tile(masked, m_halo, taps, conv, t, 1))
    loads[2].wait()

    def pair(ref, k):
        return jnp.concatenate(
            [ref[2 * k].astype(F32), ref[2 * k + 1].astype(F32)], axis=1
        )

    def gain_pair():
        return jnp.concatenate([gain_col[...], gain_col[...]], axis=1)

    def norm_step(k):
        c = conv[k]
        mu = jnp.sum(c, axis=0, keepdims=True) * (1.0 / CH)
        centered = c - mu
        var = jnp.sum(centered * centered, axis=0, keepdims=True) * (1.0 / CH)
        inv_sigma = lax.rsqrt(var + 1e-6)
        nhat = centered * inv_sigma
        inv[k] = inv_sigma
        conv[k] = nhat
        aug[k, 0:CH, :] = (nhat * gain_pair()).astype(BF16)
        gm[k] = (pair(cot, k) * pair(m3, k)).astype(BF16)

    loop(0, ROWS // 2, norm_step)

    def mlp_step(h, k):
        bias2 = jnp.concatenate([bias_col[h], bias_col[h]], axis=1)
        pre = jnp.dot(w_in_t[h], aug[k, 0:CH, :], preferred_element_type=F32) + bias2
        d_act = jnp.dot(w_out[h], gm[k], preferred_element_type=F32)
        act, slope = gelu_terms(pre)
        act = act.astype(BF16)
        d_pre = (d_act * slope).astype(BF16)
        more_branch = jnp.dot(w_out_t[h], act, preferred_element_type=F32)
        more_d = jnp.dot(w_in[h], d_pre, preferred_element_type=F32)
        if h == 0:
            branch[k] = more_branch
            d_normed[k] = more_d
        else:
            branch[k] += more_branch
            d_normed[k] += more_d
        part_in[...] += lax.dot_general(
            aug[k], d_pre, (((1,), (1,)), ((), ())), preferred_element_type=F32
        )
        part_out[...] += lax.dot_general(
            act, gm[k], (((1,), (1,)), ((), ())), preferred_element_type=F32
        )

    def exchange_half(h):
        to_sibling(h).wait()

        def add(d):
            mine = parts[h, core, d].astype(F32)
            half_sum[h, d] = (mine + sib_in[h, d].astype(F32)).astype(BF16)

        loop(0, PEERS, add)
        start_all(over_dp(h), PEERS)

    for h in range(3):
        part_in[...] = jnp.zeros_like(part_in)
        part_out[...] = jnp.zeros_like(part_out)
        loop(0, 4, functools.partial(mlp_step, h))
        if h:
            exchange_half(h - 1)
        loop(4, 8, functools.partial(mlp_step, h))
        for d in range(PEERS):
            block[0:12, :] = part_in[12 * d : 12 * d + 12, :]
            block[12:13, :] = part_in[CH : CH + 1, :]
            parts[h, 0, d] = block[...].astype(BF16)
            parts[h, 1, d, :, 0:CH] = part_out[16 * d : 16 * d + 16, :].astype(BF16)
            parts[h, 1, d, :, CH:256] = jnp.zeros((16, 64), BF16)
        to_sibling(h).start()

    def norm_back(k):
        nhat = conv[k]
        d_n = d_normed[k]
        m2 = pair(m3, k)
        result = (m2 * (pair(fields, k) + branch[k])).astype(BF16)
        along = d_n * nhat
        gain_sum[...] += along[:, :LANES] + along[:, LANES:]
        d_hat = d_n * gain_pair()
        mean_d = jnp.sum(d_hat, axis=0, keepdims=True) * (1.0 / CH)
        mean_dn = jnp.sum(d_hat * nhat, axis=0, keepdims=True) * (1.0 / CH)
        d = inv[k] * (d_hat - mean_d - nhat * mean_dn)
        for j in range(2):
            out[2 * k + j] = result[:, half(j)]
            grad[2 * k + j] = d[:, half(j)]

    loop(0, ROWS // 2, norm_back)
    store = pltpu.make_async_copy(out, out_hbm, load_sem.at[3])
    store.start()
    exchange_half(2)
    d_edges[...] = pack_edges(lambda i: grad[i]).astype(BF16)
    for k in range(2):
        grad_edge(k).start()

    loop(0, TILES, lambda t: kernel_grad_tile(masked, m_halo, grad, taps_grad, t))
    flipped = jnp.transpose(taps_grad[...])
    gain_total = jnp.sum(jnp.transpose(gain_sum[...]), axis=0, keepdims=True)
    stage[0:64, :] = flipped[0:64, :]
    stage[56:57, :] = gain_total
    for p in range(PEERS):
        k_pieces[p] = stage[4 * p : 4 * p + 4, :]
    start_all(kernel_scatter, PEERS)

    for k in range(2):
        grad_edge(k).wait()
    spread_edges(merge_edges(d_slots[1], d_slots[0]), d_halo)

    def spread_step(t):
        conv_tile(grad, d_halo, taps, branch, t, -1)

    loop(0, 8, spread_step)
    wait_all(kernel_scatter, PEERS)
    k_sum[...] = sum_slots(k_pieces[lon], k_lon, PEERS)
    start_all(kernel_over_dp, PEERS)
    for h in range(3):
        wait_all(over_dp(h), PEERS)
        dp_sum[h] = sum_slots(half_sum[h, dp], dp_in.at[h], PEERS).astype(BF16)
    start_all(over_lon, PEERS // 2)
    loop(8, 16, spread_step)
    wait_all(kernel_over_dp, PEERS)
    k_full[...] = sum_slots(k_sum[...], k_dp, PEERS)
    start_all(kernel_gather, PEERS)
    wait_all(over_lon, PEERS // 2)
    for h in range(3):
        total[h] = sum_slots(dp_sum[h], lon_in.at[:, h], PEERS // 2)
    last_sibling().start()
    loop(16, TILES, spread_step)

    for i in range(ROWS):
        m = maskf[i : i + 1, :]
        grad_fields[i] = (m * (cot[i].astype(F32) + branch[i // 2, :, half(i)])).astype(BF16)

    wait_all(kernel_gather, PEERS)
    k_all[0] = k_full[...]
    for p in range(PEERS):
        kern_total[4 * p : 4 * p + 4, :] = k_all[lax.rem(lon - p + PEERS, PEERS)]
    last_sibling().wait()
    mine, other = total[...], sib_total[...]
    even = core == 0
    totals[0] = jnp.where(even, mine, other)
    totals[1] = jnp.where(even, other, mine)
    store.wait()


def finish_kernel(
    out_in, grad_in, totals, kern_total,
    out, grad, g_in, g_out, g_gain, g_bias, g_kern,
    wide, tall, sems, *, scale
):
    copies = []
    for n in range(4):
        rows = pl.ds(4 * n, 4)
        copies.append(pltpu.make_async_copy(out_in.at[rows], out.at[rows], sems.at[n]))
        copies.append(pltpu.make_async_copy(grad_in.at[rows], grad.at[rows], sems.at[4 + n]))
    for copy in copies:
        copy.start()
    for h in range(3):
        turned = jnp.transpose(totals[0, h] * scale)
        for d in range(PEERS):
            tall[48 * d + 16 * h : 48 * d + 16 * h + 16, :] = turned[16 * d : 16 * d + 16, :]
        g_out[16 * h : 16 * h + 16, :] = totals[1, h, :, 0:CH] * scale
    wide[...] = jnp.transpose(tall[...])
    g_in[...] = wide[0:12, :]
    g_bias[...] = wide[12:13, :]
    g_gain[...] = kern_total[56:57, :] * scale
    for a in range(7):
        g_kern[a] = kern_total[8 * a : 8 * a + 7, :] * scale
    for copy in copies:
        copy.wait()


def vmem():
    return pl.BlockSpec(memory_space=pltpu.VMEM)


def anywhere():
    return pl.BlockSpec(memory_space=pl.ANY)


def per_device(fields, cotangent, land_sea, kernel, ln_gain, weight_in, bias_in, weight_out):
    x = jnp.transpose(fields, (0, 1, 3, 2)).reshape(ROWS, CH, LANES)
    cot = jnp.transpose(cotangent, (0, 1, 3, 2)).reshape(ROWS, CH, LANES)
    w_out_t = jnp.transpose(weight_out)
    dma = pltpu.SemaphoreType.DMA
    big = (ROWS, CH, LANES)
    pairs = (ROWS // 2, CH, 2 * LANES)
    piece = (4, CH)
    blk = (16, 256)

    out, grad_fields, totals, kern_total = pl.pallas_call(
        main_kernel,
        name="block_and_grads",
        out_shape=(
            jax.ShapeDtypeStruct(big, BF16),
            jax.ShapeDtypeStruct(big, BF16),
            jax.ShapeDtypeStruct((2, 3) + blk, F32),
            jax.ShapeDtypeStruct((64, CH), F32),
        ),
        in_specs=[vmem(), anywhere(), vmem(), vmem(), vmem(), anywhere(), vmem(), anywhere()],
        out_specs=(anywhere(), vmem(), vmem(), vmem()),
        scratch_shapes=[
            pltpu.VMEM(big, BF16),
            pltpu.VMEM((CH, HID), BF16),
            pltpu.VMEM((CH, HID), BF16),
            pltpu.VMEM(big, BF16),
            pltpu.VMEM(big, F32),
            pltpu.VMEM(big, F32),
            pltpu.VMEM(big, F32),
            pltpu.VMEM(big, F32),
            pltpu.VMEM(pairs, F32),
            pltpu.VMEM(pairs, F32),
            pltpu.VMEM(pairs, F32),
            pltpu.VMEM((LANES, CH), F32),
            pltpu.VMEM((CH, LANES), F32),
            pltpu.VMEM((CH, LANES), F32),
            pltpu.VMEM((ROWS, 1, LANES), F32),
            pltpu.VMEM((CH, LANES), F32),
            pltpu.VMEM((3, 256, LANES), F32),
            pltpu.VMEM((3, 256, CH), BF16),
            pltpu.VMEM((3, CH, 256), BF16),
            pltpu.VMEM((3, 256, CH), BF16),
            pltpu.VMEM((3, CH, 256), BF16),
            pltpu.VMEM((ROWS // 2, CH + 16, 2 * LANES), BF16),
            pltpu.VMEM(pairs, BF16),
            pltpu.VMEM((ROWS // 2, 1, 2 * LANES), F32),
            pltpu.VMEM((CH + 16, 256), F32),
            pltpu.VMEM((256, CH), F32),
            pltpu.VMEM((CH, LANES), F32),
            pltpu.VMEM(blk, F32),
            pltpu.VMEM((CH, LANES), BF16),
            pltpu.VMEM((2, CH, LANES), BF16),
            pltpu.VMEM((CH, LANES), BF16),
            pltpu.VMEM((2, CH, LANES), BF16),
            pltpu.VMEM((3, 2, PEERS) + blk, BF16),
            pltpu.VMEM((3, PEERS) + blk, BF16),
            pltpu.VMEM((3, PEERS) + blk, BF16),
            pltpu.VMEM((3, PEERS) + blk, BF16),
            pltpu.VMEM((3,) + blk, BF16),
            pltpu.VMEM((PEERS // 2, 3) + blk, BF16),
            pltpu.VMEM((3,) + blk, F32),
            pltpu.VMEM((3,) + blk, F32),
            pltpu.VMEM((PEERS,) + piece, F32),
            pltpu.VMEM((PEERS,) + piece, F32),
            pltpu.VMEM(piece, F32),
            pltpu.VMEM((PEERS,) + piece, F32),
            pltpu.VMEM(piece, F32),
            pltpu.VMEM((PEERS,) + piece, F32),
            dma((4,)),
            dma((2,)),
            dma((2,)),
            dma((2,)),
            dma((2,)),
            dma((3,)),
            dma((3,)),
            dma,
            dma,
            dma((3, PEERS)),
            dma((3, PEERS)),
            dma((PEERS // 2,)),
            dma((PEERS // 2,)),
            dma((PEERS,)),
            dma((PEERS,)),
            dma((PEERS,)),
            dma((PEERS,)),
            dma((PEERS,)),
            dma((PEERS,)),
        ],
        compiler_params=pltpu.CompilerParams(
            collective_id=0, has_side_effects=True, vmem_limit_bytes=VMEM_BYTES
        ),
    )(x, cot, land_sea, kernel, ln_gain.reshape(1, CH), weight_in, bias_in.reshape(1, HID), w_out_t)

    total_cells = ROWS * LANES * lax.axis_size("dp") * lax.axis_size("lon")
    out, grad_fields, g_in, g_out, g_gain, g_bias, g_kern = pl.pallas_call(
        functools.partial(finish_kernel, scale=1.0 / math.sqrt(total_cells)),
        name="finish",
        out_shape=(
            jax.ShapeDtypeStruct(big, BF16),
            jax.ShapeDtypeStruct(big, BF16),
            jax.ShapeDtypeStruct((12, HID), F32),
            jax.ShapeDtypeStruct((48, CH), F32),
            jax.ShapeDtypeStruct((1, CH), F32),
            jax.ShapeDtypeStruct((1, HID), F32),
            jax.ShapeDtypeStruct((7, 7, CH), F32),
        ),
        in_specs=[anywhere(), anywhere(), vmem(), vmem()],
        out_specs=(anywhere(), anywhere()) + (vmem(),) * 5,
        scratch_shapes=[
            pltpu.VMEM((16, HID), F32),
            pltpu.VMEM((HID, 16), F32),
            dma((8,)),
        ],
    )(out, grad_fields, totals, kern_total)

    def back(y):
        return jnp.transpose(y[None], (0, 1, 3, 2))

    return (
        back(out),
        back(grad_fields),
        g_in,
        g_out,
        g_kern,
        g_gain.reshape(CH),
        g_bias.reshape(HID),
    )


def solution(mesh):
    placed = (
        P("dp", None, "lon", None),
        P("dp", None, "lon", None),
        P(None, "lon"),
        P(),
        P(),
        P(),
        P(),
        P(),
    )
    return jax.shard_map(
        per_device,
        mesh=mesh,
        in_specs=placed,
        out_specs=(
            P("dp", None, "lon", None),
            P("dp", None, "lon", None),
            P("dp", None),
            P("dp", None),
            P(),
            P(),
            P(),
        ),
        check_vma=False,
    )
```

time: 79.5 us -> 122 us (1.53)
  Pallas kernels: 71 us -> 118 us
  local copies, waits for them, and re-layouts: 6.87 us -> 1.94 us
    pallas_call x3 -> x2, Pallas kernels: 71 us -> 118 us  [the longest x1 67.8 us: per_device(): pl.pallas_call(main_kernel, name='block_and_grads', out_shape=(jax.ShapeD...]
    unnamed x17 -> x4, local copies, waits for them, and re-layouts: 6.29 us -> 1.36 us
where the time goes in v2:
time: 122 us; the launch traced here: 121 us
  Pallas kernels  118 us (97%)
  local copies, waits for them, and re-layouts  1.94 us (2%)
    pallas_call x1, Pallas kernels, per_device(): pl.pallas_call(main_kernel, name='block_and_grads', out_shape=(jax.ShapeD...  67.8 us
    pallas_call x1, Pallas kernels, per_device(): pl.pallas_call(functools.partial(finish_kernel, scale=1.0 / math.sqrt(tot...  50.4 us

profile of v2, /device:TPU:1, one launch (start us, length us, event | category | flops | bytes accessed | tf_op | source)
XLA Modules:
  0.0 121.4 jit_solution(1708808674482987998)
XLA Ops:
  0.6 0.0 copy-start
  0.6 0.7 copy-done
  1.3 0.6 reshape.35.bias_row
  1.9 67.8 %block_and_grads.1 = (bf16[16,192,128]{2,1,0:T(8,128)(2,1)}, bf16[16,192,128]{2,1,0:T(8,128)(2,1)}, f32[2,3,16,256]{3,2,1,0:T(8,128)}, f32[64,192]{1,0:T(8,128)}) custom-call(bf16[16,192,128]{2,1,0:T(8,128)(2,1)} %bitcast.15, bf16[16,192,128]{2,1,0:T(8,128)(2,1)} %bitcast.16, s32[16,128]{1,0:T(8,128)} %mask.1, f32[7,7,192]{2,1,0:T(8,128)} %kern.1, ...), custom_call_target="tpu_custom_call" | custom-call | tf_op jit(solution)/shard_map/block_and_grads/pallas_call | solution.py:459
  69.7 50.4 %finish.1 = (bf16[16,192,128]{2,1,0:T(8,128)(2,1)}, bf16[16,192,128]{2,1,0:T(8,128)(2,1)}, f32[12,768]{1,0:T(8,128)}, f32[48,192]{1,0:T(8,128)}, f32[1,192]{1,0:...) custom-call(bf16[16,192,128]{2,1,0:T(8,128)(2,1)} %get-tuple-element.18.out_in, ...), custom_call_target="tpu_custom_call" | custom-call | tf_op jit(solution)/shard_map/finish/pallas_call | solution.py:543
  120.1 0.0 copy-start.1
  120.1 0.7 copy-done.1
  120.8 0.6 reduce
Async XLA Ops:
  0.6 0.7 copy-start
  120.1 0.7 copy-start.1

commit v3 on v2

--- a/solution.py
+++ b/solution.py
@@ -15,7 +15,9 @@
 CH = 192
 HID = 768
 LANES = 128
-TILES = CH // 8
+TILES = CH // 16
+STEP = 1024
+STEPS = ROWS * LANES // STEP
 PEERS = 16
 VMEM_BYTES = 60 * 1024 * 1024
 
@@ -26,7 +28,7 @@
 
 def pack_edges(row_of):
     group = ((lane_ids((CH, LANES)) + 4) // 8) % ROWS
-    packed = jnp.zeros((CH, LANES), F32)
+    packed = jnp.zeros((CH, LANES), BF16)
     for i in range(ROWS):
         row = row_of(i)
         if i:
@@ -36,8 +38,7 @@
 
 
 def merge_edges(from_left, from_right):
-    low = lane_ids((CH, LANES)) % 8 < 4
-    return jnp.where(low, from_right.astype(F32), from_left.astype(F32))
+    return jnp.where(lane_ids((CH, LANES)) % 8 < 4, from_right, from_left)
 
 
 def spread_edges(edges, halo_ref):
@@ -46,56 +47,69 @@
 
 
 def shifted_rows(src, halo, c0, shift):
-    lane = lane_ids((8, LANES))
+    lane = lane_ids((16, LANES))
     rows = []
     for r in range(ROWS):
-        row = src[r, pl.ds(c0, 8), :]
+        row = src[r, pl.ds(c0, 16), :]
         if shift > 0:
-            row = jnp.where(lane < shift, halo[r, pl.ds(c0, 8), :], row)
+            row = jnp.where(lane < shift, halo[r, pl.ds(c0, 16), :], row)
         elif shift < 0:
-            row = jnp.where(lane >= LANES + shift, halo[r, pl.ds(c0, 8), :], row)
+            row = jnp.where(lane >= LANES + shift, halo[r, pl.ds(c0, 16), :], row)
         if shift:
             row = pltpu.roll(row, (LANES - shift) % LANES, axis=1)
         rows.append(row)
     return rows
 
 
+def plus(total, term):
+    return term if total is None else total + term
+
+
 def conv_tile(src, halo, taps, dst, tile, sign):
-    c0 = pl.multiple_of(tile * 8, 8)
-    weights = taps[pl.ds(c0, 8), :]
-    total = [None] * ROWS
+    c0 = pl.multiple_of(tile * 16, 16)
+    weights = taps[pl.ds(c0, 16), :]
     for b in range(7):
         rows = shifted_rows(src, halo, c0, sign * (b - 3))
+        part = [None] * ROWS
         for a in range(7):
             col = 8 * a + b
-            w = jnp.broadcast_to(weights[:, col : col + 1], (8, LANES))
+            w = jnp.broadcast_to(weights[:, col : col + 1], (16, LANES)).astype(BF16)
             for i in range(ROWS):
                 r = i + sign * (a - 3)
                 if 0 <= r < ROWS:
-                    term = w * rows[r]
-                    total[i] = term if total[i] is None else total[i] + term
-    for i in range(ROWS):
-        dst[i // 2, pl.ds(c0, 8), LANES * (i % 2) : LANES * (i % 2) + LANES] = total[i]
+                    part[i] = plus(part[i], w * rows[r])
+        for i in range(ROWS):
+            if b:
+                dst[i, pl.ds(c0, 16), :] += part[i].astype(F32)
+            else:
+                dst[i, pl.ds(c0, 16), :] = part[i].astype(F32)
 
 
 def kernel_grad_tile(src, halo, grad, dst, tile):
-    c0 = pl.multiple_of(tile * 8, 8)
-    lane = lane_ids((8, LANES))
-    out = jnp.zeros((8, LANES), F32)
+    c0 = pl.multiple_of(tile * 16, 16)
     for b in range(7):
         rows = shifted_rows(src, halo, c0, b - 3)
-        sums = [None] * 7
+        sums = [[None] * 7, [None] * 7]
         for i in range(ROWS):
-            g = grad[i, pl.ds(c0, 8), :]
+            g = grad[i, pl.ds(c0, 16), :]
+            part = sums[i // 8]
             for a in range(7):
                 r = i + a - 3
                 if 0 <= r < ROWS:
-                    term = g * rows[r]
-                    sums[a] = term if sums[a] is None else sums[a] + term
+                    part[a] = plus(part[a], g * rows[r])
         for a in range(7):
-            col = jnp.sum(sums[a], axis=1, keepdims=True)
-            out = jnp.where(lane == 8 * a + b, col, out)
-    dst[pl.ds(c0, 8), :] = out
+            both = sums[0][a].astype(F32) + sums[1][a].astype(F32)
+            dst[8 * a + b, pl.ds(c0, 16), :] = both.astype(BF16)
+
+
+def sum_lanes(src):
+    lane = lane_ids((LANES, LANES))
+    total = jnp.zeros((CH, LANES), F32)
+    for a in range(7):
+        for b in range(7):
+            pick = jnp.where(lane == 8 * a + b, 1.0, 0.0).astype(BF16)
+            total = total + jnp.dot(src[8 * a + b], pick, preferred_element_type=F32)
+    return total
 
 
 def load_taps(kern_ref, stage, taps):
@@ -128,16 +142,12 @@
     lax.fori_loop(lo, hi, body, 0)
 
 
-def half(i):
-    return slice(LANES * (i % 2), LANES * (i % 2) + LANES)
-
-
 def main_kernel(
     fields, cot_hbm, mask, kern, gain_row, w_in_hbm, bias_row, w_out_t_hbm,
     out_hbm, grad_fields, totals, kern_total,
     cot, w_in_raw, w_out_t_raw, out,
     masked, m_halo, grad, d_halo, conv, branch, d_normed,
-    stage, taps, taps_grad, m3, gain_col, bias_col,
+    stage, taps, tap_sums, m3, gain_col, bias_col,
     w_in_t, w_in, w_out, w_out_t, aug, gm, inv,
     part_in, part_out, gain_sum, block,
     m_edges, m_slots, d_edges, d_slots,
@@ -235,8 +245,8 @@
     maskf = mask[...].astype(F32)
     for i in range(ROWS):
         m3[i] = maskf[i : i + 1, :]
-        masked[i] = fields[i].astype(F32) * maskf[i : i + 1, :]
-    m_edges[...] = pack_edges(lambda i: masked[i]).astype(BF16)
+        masked[i] = (fields[i].astype(F32) * maskf[i : i + 1, :]).astype(BF16)
+    m_edges[...] = pack_edges(lambda i: masked[i])
     pl.semaphore_wait(barrier, 2 * (PEERS - 1))
     for k in range(2):
         field_edge(k).start()
@@ -257,8 +267,8 @@
             bias_col[h, to, :] = bias_wide[at, :]
         w_in[h] = jnp.transpose(w_in_t[h].astype(F32)).astype(BF16)
         w_out_t[h] = jnp.transpose(w_out[h].astype(F32)).astype(BF16)
-    ones_row = lax.broadcasted_iota(jnp.int32, (16, 2 * LANES), 0) == 0
-    for k in range(ROWS // 2):
+    ones_row = lax.broadcasted_iota(jnp.int32, (16, STEP), 0) == 0
+    for k in range(STEPS):
         aug[k, CH : CH + 16, :] = jnp.where(ones_row, 1.0, 0.0).astype(BF16)
     gain_sum[...] = jnp.zeros_like(gain_sum)
     block[...] = jnp.zeros_like(block)
@@ -269,31 +279,28 @@
     loop(0, TILES, lambda t: conv_tile(masked, m_halo, taps, conv, t, 1))
     loads[2].wait()
 
-    def pair(ref, k):
-        return jnp.concatenate(
-            [ref[2 * k].astype(F32), ref[2 * k + 1].astype(F32)], axis=1
-        )
-
-    def gain_pair():
-        return jnp.concatenate([gain_col[...], gain_col[...]], axis=1)
-
-    def norm_step(k):
-        c = conv[k]
+    def place(i):
+        per = STEP // LANES
+        return i // per, pl.ds(pl.multiple_of((i % per) * LANES, LANES), LANES)
+
+    def norm_step(i):
+        k, lanes = place(i)
+        c = conv[i]
         mu = jnp.sum(c, axis=0, keepdims=True) * (1.0 / CH)
         centered = c - mu
         var = jnp.sum(centered * centered, axis=0, keepdims=True) * (1.0 / CH)
         inv_sigma = lax.rsqrt(var + 1e-6)
         nhat = centered * inv_sigma
-        inv[k] = inv_sigma
-        conv[k] = nhat
-        aug[k, 0:CH, :] = (nhat * gain_pair()).astype(BF16)
-        gm[k] = (pair(cot, k) * pair(m3, k)).astype(BF16)
-
-    loop(0, ROWS // 2, norm_step)
+        inv[i] = inv_sigma
+        conv[i] = nhat
+        aug[k, 0:CH, lanes] = (nhat * gain_col[...]).astype(BF16)
+        gm[k, :, lanes] = (cot[i].astype(F32) * m3[i]).astype(BF16)
+
+    loop(0, ROWS, norm_step)
 
     def mlp_step(h, k):
-        bias2 = jnp.concatenate([bias_col[h], bias_col[h]], axis=1)
-        pre = jnp.dot(w_in_t[h], aug[k, 0:CH, :], preferred_element_type=F32) + bias2
+        bias = jnp.concatenate([bias_col[h]] * (STEP // LANES), axis=1)
+        pre = jnp.dot(w_in_t[h], aug[k, 0:CH, :], preferred_element_type=F32) + bias
         d_act = jnp.dot(w_out[h], gm[k], preferred_element_type=F32)
         act, slope = gelu_terms(pre)
         act = act.astype(BF16)
@@ -306,12 +313,18 @@
         else:
             branch[k] += more_branch
             d_normed[k] += more_d
-        part_in[...] += lax.dot_general(
+        more_in = lax.dot_general(
             aug[k], d_pre, (((1,), (1,)), ((), ())), preferred_element_type=F32
         )
-        part_out[...] += lax.dot_general(
+        more_out = lax.dot_general(
             act, gm[k], (((1,), (1,)), ((), ())), preferred_element_type=F32
         )
+        if k == 0:
+            part_in[...] = more_in
+            part_out[...] = more_out
+        else:
+            part_in[...] += more_in
+            part_out[...] += more_out
 
     def exchange_half(h):
         to_sibling(h).wait()
@@ -324,12 +337,10 @@
         start_all(over_dp(h), PEERS)
 
     for h in range(3):
-        part_in[...] = jnp.zeros_like(part_in)
-        part_out[...] = jnp.zeros_like(part_out)
-        loop(0, 4, functools.partial(mlp_step, h))
+        mlp_step(h, 0)
         if h:
             exchange_half(h - 1)
-        loop(4, 8, functools.partial(mlp_step, h))
+        mlp_step(h, 1)
         for d in range(PEERS):
             block[0:12, :] = part_in[12 * d : 12 * d + 12, :]
             block[12:13, :] = part_in[CH : CH + 1, :]
@@ -338,31 +349,27 @@
             parts[h, 1, d, :, CH:256] = jnp.zeros((16, 64), BF16)
         to_sibling(h).start()
 
-    def norm_back(k):
-        nhat = conv[k]
-        d_n = d_normed[k]
-        m2 = pair(m3, k)
-        result = (m2 * (pair(fields, k) + branch[k])).astype(BF16)
-        along = d_n * nhat
-        gain_sum[...] += along[:, :LANES] + along[:, LANES:]
-        d_hat = d_n * gain_pair()
+    def norm_back(i):
+        k, lanes = place(i)
+        nhat = conv[i]
+        d_n = d_normed[k, :, lanes]
+        out[i] = (m3[i] * (fields[i].astype(F32) + branch[k, :, lanes])).astype(BF16)
+        gain_sum[...] += d_n * nhat
+        d_hat = d_n * gain_col[...]
         mean_d = jnp.sum(d_hat, axis=0, keepdims=True) * (1.0 / CH)
         mean_dn = jnp.sum(d_hat * nhat, axis=0, keepdims=True) * (1.0 / CH)
-        d = inv[k] * (d_hat - mean_d - nhat * mean_dn)
-        for j in range(2):
-            out[2 * k + j] = result[:, half(j)]
-            grad[2 * k + j] = d[:, half(j)]
-
-    loop(0, ROWS // 2, norm_back)
+        grad[i] = (inv[i] * (d_hat - mean_d - nhat * mean_dn)).astype(BF16)
+
+    loop(0, ROWS, norm_back)
     store = pltpu.make_async_copy(out, out_hbm, load_sem.at[3])
     store.start()
     exchange_half(2)
-    d_edges[...] = pack_edges(lambda i: grad[i]).astype(BF16)
+    d_edges[...] = pack_edges(lambda i: grad[i])
     for k in range(2):
         grad_edge(k).start()
 
-    loop(0, TILES, lambda t: kernel_grad_tile(masked, m_halo, grad, taps_grad, t))
-    flipped = jnp.transpose(taps_grad[...])
+    loop(0, TILES, lambda t: kernel_grad_tile(masked, m_halo, grad, tap_sums, t))
+    flipped = jnp.transpose(sum_lanes(tap_sums))
     gain_total = jnp.sum(jnp.transpose(gain_sum[...]), axis=0, keepdims=True)
     stage[0:64, :] = flipped[0:64, :]
     stage[56:57, :] = gain_total
@@ -375,9 +382,9 @@
     spread_edges(merge_edges(d_slots[1], d_slots[0]), d_halo)
 
     def spread_step(t):
-        conv_tile(grad, d_halo, taps, branch, t, -1)
-
-    loop(0, 8, spread_step)
+        conv_tile(grad, d_halo, taps, conv, t, -1)
+
+    loop(0, 4, spread_step)
     wait_all(kernel_scatter, PEERS)
     k_sum[...] = sum_slots(k_pieces[lon], k_lon, PEERS)
     start_all(kernel_over_dp, PEERS)
@@ -385,7 +392,7 @@
         wait_all(over_dp(h), PEERS)
         dp_sum[h] = sum_slots(half_sum[h, dp], dp_in.at[h], PEERS).astype(BF16)
     start_all(over_lon, PEERS // 2)
-    loop(8, 16, spread_step)
+    loop(4, 8, spread_step)
     wait_all(kernel_over_dp, PEERS)
     k_full[...] = sum_slots(k_sum[...], k_dp, PEERS)
     start_all(kernel_gather, PEERS)
@@ -393,11 +400,11 @@
     for h in range(3):
         total[h] = sum_slots(dp_sum[h], lon_in.at[:, h], PEERS // 2)
     last_sibling().start()
-    loop(16, TILES, spread_step)
+    loop(8, TILES, spread_step)
 
     for i in range(ROWS):
         m = maskf[i : i + 1, :]
-        grad_fields[i] = (m * (cot[i].astype(F32) + branch[i // 2, :, half(i)])).astype(BF16)
+        grad_fields[i] = (m * (cot[i].astype(F32) + conv[i])).astype(BF16)
 
     wait_all(kernel_gather, PEERS)
     k_all[0] = k_full[...]
@@ -414,15 +421,23 @@
 def finish_kernel(
     out_in, grad_in, totals, kern_total,
     out, grad, g_in, g_out, g_gain, g_bias, g_kern,
-    wide, tall, sems, *, scale
+    held, wide, tall, sems, *, scale
 ):
-    copies = []
-    for n in range(4):
-        rows = pl.ds(4 * n, 4)
-        copies.append(pltpu.make_async_copy(out_in.at[rows], out.at[rows], sems.at[n]))
-        copies.append(pltpu.make_async_copy(grad_in.at[rows], grad.at[rows], sems.at[4 + n]))
-    for copy in copies:
-        copy.start()
+    steps = []
+    for n in range(8):
+        rows = pl.ds(4 * (n % 4), 4)
+        src, dst = (out_in, out) if n < 4 else (grad_in, grad)
+        steps.append(
+            (
+                pltpu.make_async_copy(src.at[rows], held.at[n], sems.at[0, n]),
+                pltpu.make_async_copy(held.at[n], dst.at[rows], sems.at[1, n]),
+            )
+        )
+    for load, _ in steps:
+        load.start()
+    for load, save in steps:
+        load.wait()
+        save.start()
     for h in range(3):
         turned = jnp.transpose(totals[0, h] * scale)
         for d in range(PEERS):
@@ -434,8 +449,8 @@
     g_gain[...] = kern_total[56:57, :] * scale
     for a in range(7):
         g_kern[a] = kern_total[8 * a : 8 * a + 7, :] * scale
-    for copy in copies:
-        copy.wait()
+    for _, save in steps:
+        save.wait()
 
 
 def vmem():
@@ -452,7 +467,7 @@
     w_out_t = jnp.transpose(weight_out)
     dma = pltpu.SemaphoreType.DMA
     big = (ROWS, CH, LANES)
-    pairs = (ROWS // 2, CH, 2 * LANES)
+    wide = (STEPS, CH, STEP)
     piece = (4, CH)
     blk = (16, 256)
 
@@ -472,16 +487,16 @@
             pltpu.VMEM((CH, HID), BF16),
             pltpu.VMEM((CH, HID), BF16),
             pltpu.VMEM(big, BF16),
+            pltpu.VMEM(big, BF16),
+            pltpu.VMEM(big, BF16),
+            pltpu.VMEM(big, BF16),
+            pltpu.VMEM(big, BF16),
             pltpu.VMEM(big, F32),
-            pltpu.VMEM(big, F32),
-            pltpu.VMEM(big, F32),
-            pltpu.VMEM(big, F32),
-            pltpu.VMEM(pairs, F32),
-            pltpu.VMEM(pairs, F32),
-            pltpu.VMEM(pairs, F32),
+            pltpu.VMEM(wide, F32),
+            pltpu.VMEM(wide, F32),
             pltpu.VMEM((LANES, CH), F32),
             pltpu.VMEM((CH, LANES), F32),
-            pltpu.VMEM((CH, LANES), F32),
+            pltpu.VMEM((56, CH, LANES), BF16),
             pltpu.VMEM((ROWS, 1, LANES), F32),
             pltpu.VMEM((CH, LANES), F32),
             pltpu.VMEM((3, 256, LANES), F32),
@@ -489,9 +504,9 @@
             pltpu.VMEM((3, CH, 256), BF16),
             pltpu.VMEM((3, 256, CH), BF16),
             pltpu.VMEM((3, CH, 256), BF16),
-            pltpu.VMEM((ROWS // 2, CH + 16, 2 * LANES), BF16),
-            pltpu.VMEM(pairs, BF16),
-            pltpu.VMEM((ROWS // 2, 1, 2 * LANES), F32),
+            pltpu.VMEM((STEPS, CH + 16, STEP), BF16),
+            pltpu.VMEM(wide, BF16),
+            pltpu.VMEM((ROWS, 1, LANES), F32),
             pltpu.VMEM((CH + 16, 256), F32),
             pltpu.VMEM((256, CH), F32),
             pltpu.VMEM((CH, LANES), F32),
@@ -555,9 +570,10 @@
         in_specs=[anywhere(), anywhere(), vmem(), vmem()],
         out_specs=(anywhere(), anywhere()) + (vmem(),) * 5,
         scratch_shapes=[
+            pltpu.VMEM((8, 4, CH, LANES), BF16),
             pltpu.VMEM((16, HID), F32),
             pltpu.VMEM((HID, 16), F32),
-            dma((8,)),
+            dma((2, 8)),
         ],
     )(out, grad_fields, totals, kern_total)
 

time: 122 us -> 64 us (0.52)
  Pallas kernels: 118 us -> 60.6 us
    pallas_call x1, Pallas kernels: 50.4 us -> 3.85 us  [per_device(): pl.pallas_call(functools.partial(finish_kernel, scale=1.0 / math.sqrt(tot...]
    pallas_call x1, Pallas kernels: 67.8 us -> 56.7 us  [per_device(): pl.pallas_call(main_kernel, name='block_and_grads', out_shape=(jax.ShapeD...]
where the time goes in v3:
time: 64 us; the launch traced here: 63.8 us
  Pallas kernels  60.6 us (95%)
  local copies, waits for them, and re-layouts  1.94 us (3%)
  between operations  0.67 us (1%)
    pallas_call x1, Pallas kernels, per_device(): pl.pallas_call(main_kernel, name='block_and_grads', out_shape=(jax.ShapeD...  56.7 us
    pallas_call x1, Pallas kernels, per_device(): pl.pallas_call(functools.partial(finish_kernel, scale=1.0 / math.sqrt(tot...  3.85 us
    unnamed x4, local copies, waits for them, and re-layouts  1.36 us

profile of v3, /device:TPU:1, one launch (start us, length us, event | category | flops | bytes accessed | tf_op | source)
XLA Modules:
  0.0 63.8 jit_solution(1388859678855176867)
XLA Ops:
  0.6 0.0 copy-start
  0.6 0.7 %copy-done = f32[768]{0:T(1024)S(1)} copy-done((f32[768]{0:T(1024)S(1)}, f32[768]{0:T(1024)}, u32[]{:S(2)}) %copy-start) | copy-done | bytes 3096
  1.3 0.6 reshape.35.bias_row
  1.9 56.7 %block_and_grads.1 = (bf16[16,192,128]{2,1,0:T(8,128)(2,1)}, bf16[16,192,128]{2,1,0:T(8,128)(2,1)}, f32[2,3,16,256]{3,2,1,0:T(8,128)}, f32[64,192]{1,0:T(8,128)}) custom-call(bf16[16,192,128]{2,1,0:T(8,128)(2,1)} %bitcast.15, bf16[16,192,128]{2,1,0:T(8,128)(2,1)} %bitcast.16, s32[16,128]{1,0:T(8,128)} %mask.1, f32[7,7,192]{2,1,0:T(8,128)} %kern.1, ...), custom_call_target="tpu_custom_call" | custom-call | tf_op jit(solution)/shard_map/block_and_grads/pallas_call | solution.py:474
  58.6 3.9 %finish.1 = (bf16[16,192,128]{2,1,0:T(8,128)(2,1)}, bf16[16,192,128]{2,1,0:T(8,128)(2,1)}, f32[12,768]{1,0:T(8,128)}, f32[48,192]{1,0:T(8,128)}, f32[1,192]{1,0:...) custom-call(bf16[16,192,128]{2,1,0:T(8,128)(2,1)} %get-tuple-element.18.out_in, ...), custom_call_target="tpu_custom_call" | custom-call | tf_op jit(solution)/shard_map/finish/pallas_call | solution.py:558
  62.5 0.0 copy-start.1
  62.5 0.7 %copy-done.1 = f32[1,768]{1,0:T(1,128)S(1)} copy-done((f32[1,768]{1,0:T(1,128)S(1)}, f32[1,768]{1,0:T(1,128)}, u32[]{:S(2)}) %copy-start.1) | copy-done | bytes 3096
  63.2 0.6 reduce
Async XLA Ops:
  0.6 0.7 %copy-start = (f32[768]{0:T(1024)S(1)}, f32[768]{0:T(1024)}, u32[]{:S(2)}) copy-start(f32[768]{0:T(1024)} %param.14) | copy-start | bytes 9220
  62.5 0.7 %copy-start.1 = (f32[1,768]{1,0:T(1,128)S(1)}, f32[1,768]{1,0:T(1,128)}, u32[]{:S(2)}) copy-start(f32[1,768]{1,0:T(1,128)} %get-tuple-element.28) | copy-start | bytes 9220

commit v4 on v3

--- a/solution.py
+++ b/solution.py
@@ -146,14 +146,14 @@
     fields, cot_hbm, mask, kern, gain_row, w_in_hbm, bias_row, w_out_t_hbm,
     out_hbm, grad_fields, totals, kern_total,
     cot, w_in_raw, w_out_t_raw, out,
-    masked, m_halo, grad, d_halo, conv, branch, d_normed,
+    masked, m_halo, grad, d_halo, conv, acts, d_normed,
     stage, taps, tap_sums, m3, gain_col, bias_col,
     w_in_t, w_in, w_out, w_out_t, aug, gm, inv,
     part_in, part_out, gain_sum, block,
     m_edges, m_slots, d_edges, d_slots,
-    parts, sib_in, half_sum, dp_in, dp_sum, lon_in, total, sib_total,
+    parts, sib_in, half_sum, dp_in, dp_sum, lon_in,
     k_pieces, k_lon, k_sum, k_dp, k_full, k_all,
-    load_sem, m_send, m_recv, d_send, d_recv, sib_send, sib_recv, last_send, last_recv,
+    load_sem, m_send, m_recv, d_send, d_recv, sib_send, sib_recv,
     dp_send, dp_recv, lon_send, lon_recv,
     ks_send, ks_recv, kd_send, kd_recv, kg_send, kg_recv,
 ):
@@ -197,34 +197,36 @@
         def make(k):
             return remote(
                 half_sum.at[h, lax.rem(dp + k, PEERS)], dp_in.at[h, k],
-                dp_send.at[h, k], dp_recv.at[h, k], dp_peer(k),
+                dp_send.at[h], dp_recv.at[h], dp_peer(k),
             )
 
         return make
 
-    def over_lon(k):
-        return remote(dp_sum, lon_in.at[k], lon_send.at[k], lon_recv.at[k], lon_peer(2 * k))
-
-    def last_sibling():
-        return remote(total, sib_total, last_send, last_recv, lon_device(sibling))
+    def over_lon(h):
+        def make(k):
+            return remote(
+                dp_sum.at[h], lon_in.at[h, k], lon_send.at[h], lon_recv.at[h], lon_peer(k)
+            )
+
+        return make
 
     def kernel_scatter(k):
         return remote(
-            k_pieces.at[lax.rem(lon + k, PEERS)], k_lon.at[k], ks_send.at[k], ks_recv.at[k],
-            lon_peer(k),
+            k_pieces.at[lax.rem(lon + k, PEERS)], k_lon.at[k], ks_send, ks_recv, lon_peer(k)
         )
 
     def kernel_over_dp(k):
-        return remote(k_sum, k_dp.at[k], kd_send.at[k], kd_recv.at[k], dp_peer(k))
+        return remote(k_sum, k_dp.at[k], kd_send, kd_recv, dp_peer(k))
 
     def kernel_gather(k):
-        return remote(k_full, k_all.at[k], kg_send.at[k], kg_recv.at[k], lon_peer(k))
-
-    def start_all(make, count):
-        loop(1, count, lambda k: make(k).start())
-
-    def wait_all(make, count):
-        loop(1, count, lambda k: make(k).wait())
+        return remote(k_full, k_all.at[k], kg_send, kg_recv, lon_peer(k))
+
+    def start_all(make):
+        loop(1, PEERS, lambda k: make(k).start())
+
+    def wait_all(slots, sem):
+        rows = slots.at[pl.ds(1, PEERS - 1)]
+        pltpu.make_async_copy(rows, rows, sem).wait()
 
     def sum_slots(own, slots, count):
         def body(k, acc):
@@ -274,7 +276,7 @@
     block[...] = jnp.zeros_like(block)
 
     for k in range(2):
-        field_edge(k).wait()
+        field_edge(k).wait_recv()
     spread_edges(merge_edges(m_slots[1], m_slots[0]), m_halo)
     loop(0, TILES, lambda t: conv_tile(masked, m_halo, taps, conv, t, 1))
     loads[2].wait()
@@ -305,13 +307,11 @@
         act, slope = gelu_terms(pre)
         act = act.astype(BF16)
         d_pre = (d_act * slope).astype(BF16)
-        more_branch = jnp.dot(w_out_t[h], act, preferred_element_type=F32)
+        acts[h, k] = act
         more_d = jnp.dot(w_in[h], d_pre, preferred_element_type=F32)
         if h == 0:
-            branch[k] = more_branch
             d_normed[k] = more_d
         else:
-            branch[k] += more_branch
             d_normed[k] += more_d
         more_in = lax.dot_general(
             aug[k], d_pre, (((1,), (1,)), ((), ())), preferred_element_type=F32
@@ -327,14 +327,19 @@
             part_out[...] += more_out
 
     def exchange_half(h):
-        to_sibling(h).wait()
+        to_sibling(h).wait_recv()
 
         def add(d):
             mine = parts[h, core, d].astype(F32)
             half_sum[h, d] = (mine + sib_in[h, d].astype(F32)).astype(BF16)
 
         loop(0, PEERS, add)
-        start_all(over_dp(h), PEERS)
+        start_all(over_dp(h))
+
+    def exchange_sum(h):
+        wait_all(dp_in.at[h], dp_recv.at[h])
+        dp_sum[h] = sum_slots(half_sum[h, dp], dp_in.at[h], PEERS).astype(BF16)
+        start_all(over_lon(h))
 
     for h in range(3):
         mlp_step(h, 0)
@@ -353,7 +358,6 @@
         k, lanes = place(i)
         nhat = conv[i]
         d_n = d_normed[k, :, lanes]
-        out[i] = (m3[i] * (fields[i].astype(F32) + branch[k, :, lanes])).astype(BF16)
         gain_sum[...] += d_n * nhat
         d_hat = d_n * gain_col[...]
         mean_d = jnp.sum(d_hat, axis=0, keepdims=True) * (1.0 / CH)
@@ -361,60 +365,83 @@
         grad[i] = (inv[i] * (d_hat - mean_d - nhat * mean_dn)).astype(BF16)
 
     loop(0, ROWS, norm_back)
-    store = pltpu.make_async_copy(out, out_hbm, load_sem.at[3])
-    store.start()
     exchange_half(2)
     d_edges[...] = pack_edges(lambda i: grad[i])
     for k in range(2):
         grad_edge(k).start()
 
-    loop(0, TILES, lambda t: kernel_grad_tile(masked, m_halo, grad, tap_sums, t))
+    def kernel_step(t):
+        kernel_grad_tile(masked, m_halo, grad, tap_sums, t)
+
+    def spread_step(t):
+        conv_tile(grad, d_halo, taps, conv, t, -1)
+
+    def branch_step(k):
+        branch = jnp.zeros((CH, STEP), F32)
+        for h in range(3):
+            branch = branch + jnp.dot(w_out_t[h], acts[h, k], preferred_element_type=F32)
+        per = STEP // LANES
+        for j in range(per):
+            i = per * k + j
+            kept = fields[i].astype(F32) + branch[:, LANES * j : LANES * j + LANES]
+            out[i] = (m3[i] * kept).astype(BF16)
+
+    loop(0, TILES, kernel_step)
     flipped = jnp.transpose(sum_lanes(tap_sums))
     gain_total = jnp.sum(jnp.transpose(gain_sum[...]), axis=0, keepdims=True)
     stage[0:64, :] = flipped[0:64, :]
     stage[56:57, :] = gain_total
     for p in range(PEERS):
         k_pieces[p] = stage[4 * p : 4 * p + 4, :]
-    start_all(kernel_scatter, PEERS)
-
+    start_all(kernel_scatter)
+
+    exchange_sum(0)
+    branch_step(0)
+    exchange_sum(1)
+    branch_step(1)
+    store = pltpu.make_async_copy(out, out_hbm, load_sem.at[3])
+    store.start()
     for k in range(2):
-        grad_edge(k).wait()
+        grad_edge(k).wait_recv()
     spread_edges(merge_edges(d_slots[1], d_slots[0]), d_halo)
-
-    def spread_step(t):
-        conv_tile(grad, d_halo, taps, conv, t, -1)
-
+    wait_all(k_lon, ks_recv)
+    k_sum[...] = sum_slots(k_pieces[lon], k_lon, PEERS)
+    start_all(kernel_over_dp)
     loop(0, 4, spread_step)
-    wait_all(kernel_scatter, PEERS)
-    k_sum[...] = sum_slots(k_pieces[lon], k_lon, PEERS)
-    start_all(kernel_over_dp, PEERS)
-    for h in range(3):
-        wait_all(over_dp(h), PEERS)
-        dp_sum[h] = sum_slots(half_sum[h, dp], dp_in.at[h], PEERS).astype(BF16)
-    start_all(over_lon, PEERS // 2)
-    loop(4, 8, spread_step)
-    wait_all(kernel_over_dp, PEERS)
+    exchange_sum(2)
+    loop(4, TILES, spread_step)
+    wait_all(k_dp, kd_recv)
     k_full[...] = sum_slots(k_sum[...], k_dp, PEERS)
-    start_all(kernel_gather, PEERS)
-    wait_all(over_lon, PEERS // 2)
-    for h in range(3):
-        total[h] = sum_slots(dp_sum[h], lon_in.at[:, h], PEERS // 2)
-    last_sibling().start()
-    loop(8, TILES, spread_step)
+    start_all(kernel_gather)
 
     for i in range(ROWS):
         m = maskf[i : i + 1, :]
         grad_fields[i] = (m * (cot[i].astype(F32) + conv[i])).astype(BF16)
 
-    wait_all(kernel_gather, PEERS)
+    even = core == 0
+    for h in range(3):
+        wait_all(lon_in.at[h], lon_recv.at[h])
+        mine = dp_sum[h].astype(F32)
+        other = lon_in[h, 1].astype(F32)
+        for k in range(2, PEERS, 2):
+            mine = mine + lon_in[h, k].astype(F32)
+            other = other + lon_in[h, k + 1].astype(F32)
+        totals[0, h] = jnp.where(even, mine, other)
+        totals[1, h] = jnp.where(even, other, mine)
+    wait_all(k_all, kg_recv)
     k_all[0] = k_full[...]
     for p in range(PEERS):
         kern_total[4 * p : 4 * p + 4, :] = k_all[lax.rem(lon - p + PEERS, PEERS)]
-    last_sibling().wait()
-    mine, other = total[...], sib_total[...]
-    even = core == 0
-    totals[0] = jnp.where(even, mine, other)
-    totals[1] = jnp.where(even, other, mine)
+    for k in range(2):
+        field_edge(k).wait_send()
+        grad_edge(k).wait_send()
+    for h in range(3):
+        to_sibling(h).wait_send()
+        wait_all(dp_in.at[h], dp_send.at[h])
+        wait_all(lon_in.at[h], lon_send.at[h])
+    wait_all(k_lon, ks_send)
+    wait_all(k_dp, kd_send)
+    wait_all(k_all, kg_send)
     store.wait()
 
 
@@ -492,7 +519,7 @@
             pltpu.VMEM(big, BF16),
             pltpu.VMEM(big, BF16),
             pltpu.VMEM(big, F32),
-            pltpu.VMEM(wide, F32),
+            pltpu.VMEM((3, STEPS, 256, STEP), BF16),
             pltpu.VMEM(wide, F32),
             pltpu.VMEM((LANES, CH), F32),
             pltpu.VMEM((CH, LANES), F32),
@@ -520,9 +547,7 @@
             pltpu.VMEM((3, PEERS) + blk, BF16),
             pltpu.VMEM((3, PEERS) + blk, BF16),
             pltpu.VMEM((3,) + blk, BF16),
-            pltpu.VMEM((PEERS // 2, 3) + blk, BF16),
-            pltpu.VMEM((3,) + blk, F32),
-            pltpu.VMEM((3,) + blk, F32),
+            pltpu.VMEM((3, PEERS) + blk, BF16),
             pltpu.VMEM((PEERS,) + piece, F32),
             pltpu.VMEM((PEERS,) + piece, F32),
             pltpu.VMEM(piece, F32),
@@ -536,18 +561,16 @@
             dma((2,)),
             dma((3,)),
             dma((3,)),
+            dma((3,)),
+            dma((3,)),
+            dma((3,)),
+            dma((3,)),
             dma,
             dma,
-            dma((3, PEERS)),
-            dma((3, PEERS)),
-            dma((PEERS // 2,)),
-            dma((PEERS // 2,)),
-            dma((PEERS,)),
-            dma((PEERS,)),
-            dma((PEERS,)),
-            dma((PEERS,)),
-            dma((PEERS,)),
-            dma((PEERS,)),
+            dma,
+            dma,
+            dma,
+            dma,
         ],
         compiler_params=pltpu.CompilerParams(
             collective_id=0, has_side_effects=True, vmem_limit_bytes=VMEM_BYTES

time: 64 us -> 62.1 us (0.970)
  Pallas kernels: 60.6 us -> 58.7 us
    pallas_call x1, Pallas kernels: 56.7 us -> 54.9 us  [per_device(): pl.pallas_call(main_kernel, name='block_and_grads', out_shape=(jax.ShapeD...]
where the time goes in v4:
time: 62.1 us; the launch traced here: 61.9 us
  Pallas kernels  58.7 us (95%)
  local copies, waits for them, and re-layouts  1.94 us (3%)
  between operations  0.67 us (1%)
    pallas_call x1, Pallas kernels, per_device(): pl.pallas_call(main_kernel, name='block_and_grads', out_shape=(jax.ShapeD...  54.9 us
    pallas_call x1, Pallas kernels, per_device(): pl.pallas_call(functools.partial(finish_kernel, scale=1.0 / math.sqrt(tot...  3.85 us
    unnamed x4, local copies, waits for them, and re-layouts  1.36 us

profile of v4, /device:TPU:1, one launch (start us, length us, event | category | flops | bytes accessed | tf_op | source)
XLA Modules:
  0.0 61.9 jit_solution(13117203337298397766)
XLA Ops:
  0.6 0.0 copy-start
  0.6 0.7 %copy-done = f32[768]{0:T(1024)S(1)} copy-done((f32[768]{0:T(1024)S(1)}, f32[768]{0:T(1024)}, u32[]{:S(2)}) %copy-start) | copy-done | bytes 3096
  1.3 0.6 reshape.35.bias_row
  1.9 54.9 %block_and_grads.1 = (bf16[16,192,128]{2,1,0:T(8,128)(2,1)}, bf16[16,192,128]{2,1,0:T(8,128)(2,1)}, f32[2,3,16,256]{3,2,1,0:T(8,128)}, f32[64,192]{1,0:T(8,128)}) custom-call(bf16[16,192,128]{2,1,0:T(8,128)(2,1)} %bitcast.15, bf16[16,192,128]{2,1,0:T(8,128)(2,1)} %bitcast.16, s32[16,128]{1,0:T(8,128)} %mask.1, f32[7,7,192]{2,1,0:T(8,128)} %kern.1, ...), custom_call_target="tpu_custom_call" | custom-call | tf_op jit(solution)/shard_map/block_and_grads/pallas_call | solution.py:501
  56.8 3.9 %finish.1 = (bf16[16,192,128]{2,1,0:T(8,128)(2,1)}, bf16[16,192,128]{2,1,0:T(8,128)(2,1)}, f32[12,768]{1,0:T(8,128)}, f32[48,192]{1,0:T(8,128)}, f32[1,192]{1,0:...) custom-call(bf16[16,192,128]{2,1,0:T(8,128)(2,1)} %get-tuple-element.18.out_in, ...), custom_call_target="tpu_custom_call" | custom-call | tf_op jit(solution)/shard_map/finish/pallas_call | solution.py:581
  60.6 0.0 copy-start.1
  60.6 0.7 %copy-done.1 = f32[1,768]{1,0:T(1,128)S(1)} copy-done((f32[1,768]{1,0:T(1,128)S(1)}, f32[1,768]{1,0:T(1,128)}, u32[]{:S(2)}) %copy-start.1) | copy-done | bytes 3096
  61.3 0.6 reduce
Async XLA Ops:
  0.6 0.7 %copy-start = (f32[768]{0:T(1024)S(1)}, f32[768]{0:T(1024)}, u32[]{:S(2)}) copy-start(f32[768]{0:T(1024)} %param.14) | copy-start | bytes 9220
  60.6 0.7 %copy-start.1 = (f32[1,768]{1,0:T(1,128)S(1)}, f32[1,768]{1,0:T(1,128)}, u32[]{:S(2)}) copy-start(f32[1,768]{1,0:T(1,128)} %get-tuple-element.28) | copy-start | bytes 9220

commit v5 on v4

--- a/solution.py
+++ b/solution.py
@@ -255,7 +255,7 @@
 
     load_taps(kern, stage, taps)
     gain_col[...] = jnp.transpose(jnp.broadcast_to(gain_row[...], (LANES, CH)))
-    bias_wide = jnp.transpose(jnp.broadcast_to(bias_row[...], (LANES, HID)))
+    bias_wide = jnp.transpose(jnp.broadcast_to(bias_row[...][None, :], (LANES, HID)))
     loads[0].wait()
     loads[1].wait()
     in_t = jnp.transpose(w_in_raw[...].astype(F32)).astype(BF16)
@@ -472,7 +472,7 @@
         g_out[16 * h : 16 * h + 16, :] = totals[1, h, :, 0:CH] * scale
     wide[...] = jnp.transpose(tall[...])
     g_in[...] = wide[0:12, :]
-    g_bias[...] = wide[12:13, :]
+    g_bias[...] = wide[12, :]
     g_gain[...] = kern_total[56:57, :] * scale
     for a in range(7):
         g_kern[a] = kern_total[8 * a : 8 * a + 7, :] * scale
@@ -575,7 +575,7 @@
         compiler_params=pltpu.CompilerParams(
             collective_id=0, has_side_effects=True, vmem_limit_bytes=VMEM_BYTES
         ),
-    )(x, cot, land_sea, kernel, ln_gain.reshape(1, CH), weight_in, bias_in.reshape(1, HID), w_out_t)
+    )(x, cot, land_sea, kernel, ln_gain.reshape(1, CH), weight_in, bias_in, w_out_t)
 
     total_cells = ROWS * LANES * lax.axis_size("dp") * lax.axis_size("lon")
     out, grad_fields, g_in, g_out, g_gain, g_bias, g_kern = pl.pallas_call(
@@ -587,7 +587,7 @@
             jax.ShapeDtypeStruct((12, HID), F32),
             jax.ShapeDtypeStruct((48, CH), F32),
             jax.ShapeDtypeStruct((1, CH), F32),
-            jax.ShapeDtypeStruct((1, HID), F32),
+            jax.ShapeDtypeStruct((HID,), F32),
             jax.ShapeDtypeStruct((7, 7, CH), F32),
         ),
         in_specs=[anywhere(), anywhere(), vmem(), vmem()],
@@ -610,7 +610,7 @@
         g_out,
         g_kern,
         g_gain.reshape(CH),
-        g_bias.reshape(HID),
+        g_bias,
     )
 
 

time: 62.1 us -> 59.7 us (0.961)
  local copies, waits for them, and re-layouts: 1.94 us -> 0 us
    unnamed x4 -> x0, local copies, waits for them, and re-layouts: 1.36 us -> none
where the time goes in v5:
time: 59.7 us; the launch traced here: 59.5 us
  Pallas kernels  58.8 us (98%)
  between operations  0.64 us (1%)
    pallas_call x1, Pallas kernels, per_device(): pl.pallas_call(main_kernel, name='block_and_grads', out_shape=(jax.ShapeD...  55 us
    pallas_call x1, Pallas kernels, per_device(): pl.pallas_call(functools.partial(finish_kernel, scale=1.0 / math.sqrt(tot...  3.85 us

profile of v5, /device:TPU:1, one launch (start us, length us, event | category | flops | bytes accessed | tf_op | source)
XLA Modules:
  0.0 59.5 jit_solution(13937221343164757396)
XLA Ops:
  0.6 55.0 %block_and_grads.1 = (bf16[16,192,128]{2,1,0:T(8,128)(2,1)}, bf16[16,192,128]{2,1,0:T(8,128)(2,1)}, f32[2,3,16,256]{3,2,1,0:T(8,128)}, f32[64,192]{1,0:T(8,128)}) custom-call(bf16[16,192,128]{2,1,0:T(8,128)(2,1)} %bitcast.15, bf16[16,192,128]{2,1,0:T(8,128)(2,1)} %bitcast.16, s32[16,128]{1,0:T(8,128)} %mask.1, f32[7,7,192]{2,1,0:T(8,128)} %kern.1, ...), custom_call_target="tpu_custom_call" | custom-call | tf_op jit(solution)/shard_map/block_and_grads/pallas_call | solution.py:501
  55.6 3.9 %finish.1 = (bf16[16,192,128]{2,1,0:T(8,128)(2,1)}, bf16[16,192,128]{2,1,0:T(8,128)(2,1)}, f32[12,768]{1,0:T(8,128)}, f32[48,192]{1,0:T(8,128)}, f32[1,192]{1,0:...) custom-call(bf16[16,192,128]{2,1,0:T(8,128)(2,1)} %get-tuple-element.18.out_in, ...), custom_call_target="tpu_custom_call" | custom-call | tf_op jit(solution)/shard_map/finish/pallas_call | solution.py:581

commit v6 on v5

--- a/solution.py
+++ b/solution.py
@@ -68,6 +68,7 @@
 def conv_tile(src, halo, taps, dst, tile, sign):
     c0 = pl.multiple_of(tile * 16, 16)
     weights = taps[pl.ds(c0, 16), :]
+    total = [None] * ROWS
     for b in range(7):
         rows = shifted_rows(src, halo, c0, sign * (b - 3))
         part = [None] * ROWS
@@ -79,10 +80,9 @@
                 if 0 <= r < ROWS:
                     part[i] = plus(part[i], w * rows[r])
         for i in range(ROWS):
-            if b:
-                dst[i, pl.ds(c0, 16), :] += part[i].astype(F32)
-            else:
-                dst[i, pl.ds(c0, 16), :] = part[i].astype(F32)
+            total[i] = plus(total[i], part[i].astype(F32))
+    for i in range(ROWS):
+        dst[i, pl.ds(c0, 16), :] = total[i]
 
 
 def kernel_grad_tile(src, halo, grad, dst, tile):
@@ -242,7 +242,9 @@
     ]
     for load in loads:
         load.start()
-    loop(1, PEERS, greet)
+    greet(1)
+    greet(PEERS - 1)
+    loop(2, PEERS - 1, greet)
 
     maskf = mask[...].astype(F32)
     for i in range(ROWS):
@@ -274,16 +276,26 @@
         aug[k, CH : CH + 16, :] = jnp.where(ones_row, 1.0, 0.0).astype(BF16)
     gain_sum[...] = jnp.zeros_like(gain_sum)
     block[...] = jnp.zeros_like(block)
+    loads[2].wait()
+    per_step = STEP // LANES
+    for i in range(ROWS):
+        lanes = slice(LANES * (i % per_step), LANES * (i % per_step) + LANES)
+        gm[i // per_step, :, lanes] = (cot[i].astype(F32) * m3[i]).astype(BF16)
 
     for k in range(2):
         field_edge(k).wait_recv()
     spread_edges(merge_edges(m_slots[1], m_slots[0]), m_halo)
     loop(0, TILES, lambda t: conv_tile(masked, m_halo, taps, conv, t, 1))
-    loads[2].wait()
-
     def place(i):
         per = STEP // LANES
         return i // per, pl.ds(pl.multiple_of((i % per) * LANES, LANES), LANES)
+
+    def by_four(step):
+        def group(g):
+            for u in range(4):
+                step(4 * g + u)
+
+        return group
 
     def norm_step(i):
         k, lanes = place(i)
@@ -296,9 +308,8 @@
         inv[i] = inv_sigma
         conv[i] = nhat
         aug[k, 0:CH, lanes] = (nhat * gain_col[...]).astype(BF16)
-        gm[k, :, lanes] = (cot[i].astype(F32) * m3[i]).astype(BF16)
-
-    loop(0, ROWS, norm_step)
+
+    loop(0, ROWS // 4, by_four(norm_step))
 
     def mlp_step(h, k):
         bias = jnp.concatenate([bias_col[h]] * (STEP // LANES), axis=1)
@@ -364,7 +375,7 @@
         mean_dn = jnp.sum(d_hat * nhat, axis=0, keepdims=True) * (1.0 / CH)
         grad[i] = (inv[i] * (d_hat - mean_d - nhat * mean_dn)).astype(BF16)
 
-    loop(0, ROWS, norm_back)
+    loop(0, ROWS // 4, by_four(norm_back))
     exchange_half(2)
     d_edges[...] = pack_edges(lambda i: grad[i])
     for k in range(2):

time: 59.7 us -> 58.6 us (0.982)
  Pallas kernels: 58.8 us -> 57.8 us
    pallas_call x1, Pallas kernels: 55 us -> 54 us  [per_device(): pl.pallas_call(main_kernel, name='block_and_grads', out_shape=(jax.ShapeD...]
where the time goes in v6:
time: 58.6 us; the launch traced here: 58.5 us
  Pallas kernels  57.8 us (99%)
  between operations  0.64 us (1%)
    pallas_call x1, Pallas kernels, per_device(): pl.pallas_call(main_kernel, name='block_and_grads', out_shape=(jax.ShapeD...  54 us
    pallas_call x1, Pallas kernels, per_device(): pl.pallas_call(functools.partial(finish_kernel, scale=1.0 / math.sqrt(tot...  3.85 us

profile of v6, /device:TPU:1, one launch (start us, length us, event | category | flops | bytes accessed | tf_op | source)
XLA Modules:
  0.0 58.5 jit_solution(94461340638522966)
XLA Ops:
  0.6 54.0 %block_and_grads.1 = (bf16[16,192,128]{2,1,0:T(8,128)(2,1)}, bf16[16,192,128]{2,1,0:T(8,128)(2,1)}, f32[2,3,16,256]{3,2,1,0:T(8,128)}, f32[64,192]{1,0:T(8,128)}) custom-call(bf16[16,192,128]{2,1,0:T(8,128)(2,1)} %bitcast.15, bf16[16,192,128]{2,1,0:T(8,128)(2,1)} %bitcast.16, s32[16,128]{1,0:T(8,128)} %mask.1, f32[7,7,192]{2,1,0:T(8,128)} %kern.1, ...), custom_call_target="tpu_custom_call" | custom-call | tf_op jit(solution)/shard_map/block_and_grads/pallas_call | solution.py:512
  54.6 3.9 %finish.1 = (bf16[16,192,128]{2,1,0:T(8,128)(2,1)}, bf16[16,192,128]{2,1,0:T(8,128)(2,1)}, f32[12,768]{1,0:T(8,128)}, f32[48,192]{1,0:T(8,128)}, f32[1,192]{1,0:...) custom-call(bf16[16,192,128]{2,1,0:T(8,128)(2,1)} %get-tuple-element.18.out_in, ...), custom_call_target="tpu_custom_call" | custom-call | tf_op jit(solution)/shard_map/finish/pallas_call | solution.py:592
